TPU v7x, 256 devices: a whole 4x4x8 slice. The times are simulated.
256 devices in a mesh: row: 32 (over y, x, core), col: 8 (over z).
Axes of the slice: x: 4, y: 4, z: 8, core: 2. Of those that a mesh axis runs over, the one named last changes fastest.
Arguments:
- relief: float32 [3, 8192, 8192], P(None, 'row', 'col'), may hold values from -8 to 8
Outputs:
- level_one: float32 [3, 4096, 4096], P(None, 'row', 'col')
- level_two: float32 [3, 2048, 2048], P(None, 'row', 'col')
- level_three: float32 [3, 1024, 1024], P(None, 'row', 'col')
- level_four: float32 [3, 512, 512], P(None, 'row', 'col')
All inputs are finite; a program needn't handle non-finite values.
Results may differ from a plain program's by a relative error of at most 0.00002.
Values sent between devices are 32-bit elements; how exact they have to be, the bound alone decides.
A program may use at most 64 MiB of HBM per device.

v0:
```python
import jax
import jax.numpy as jnp
from jax import lax
from jax.sharding import PartitionSpec as P

binomial = (0.0625, 0.25, 0.375, 0.25, 0.0625)
margin = 2
coarse_margins = (6, 2)


def padded_2(cells, sides, width):
    for axis, dim in sides:
        count = lax.axis_size(axis)
        ends = count - 1
        head = lax.slice_in_dim(cells, 0, width, axis=dim)
        tail = lax.slice_in_dim(cells, cells.shape[dim] - width, cells.shape[dim], axis=dim)
        cells = jnp.concatenate(
            [
                lax.ppermute(tail, axis, [(i, (i + 1) % count) for i in range(ends)]),
                cells,
                lax.ppermute(head, axis, [((i + 1) % count, i) for i in range(ends)]),
            ],
            axis=dim,
        )
    return cells


def decimate(padded, along, extent):
    result = binomial[0] * lax.slice_in_dim(padded, 0, extent - 1, 2, along)
    for offset in range(1, 5):
        result = result + binomial[offset] * lax.slice_in_dim(
            padded, offset, offset + extent - 1, 2, along
        )
    return result


def decimate_count(padded, along, count):
    result = binomial[0] * lax.slice_in_dim(padded, 0, 2 * count - 1, 2, along)
    for offset in range(1, 5):
        result = result + binomial[offset] * lax.slice_in_dim(
            padded, offset, offset + 2 * count - 1, 2, along
        )
    return result


def reflect_edges(padded, along, position, final_index, extent):
    upper = jnp.flip(lax.slice_in_dim(padded, margin + 1, 2 * margin + 1, 1, along), along)
    lower = jnp.flip(lax.slice_in_dim(padded, extent - 1, extent + margin - 1, 1, along), along)
    inside = lax.slice_in_dim(padded, margin, margin + extent, 1, along)
    sent_upper = lax.slice_in_dim(padded, 0, margin, 1, along)
    sent_lower = lax.slice_in_dim(padded, margin + extent, 2 * margin + extent, 1, along)
    upper = jnp.where(position == 0, upper, sent_upper)
    lower = jnp.where(position == final_index, lower, sent_lower)
    return jnp.concatenate([upper, inside, lower], along)


def reflect_deep(padded, along, position, final_index, extent, width):
    upper = jnp.flip(lax.slice_in_dim(padded, width + 1, 2 * width + 1, 1, along), along)
    lower = jnp.flip(
        lax.slice_in_dim(padded, width + extent - 1 - width, width + extent - 1, 1, along), along
    )
    inside = lax.slice_in_dim(padded, width, width + extent, 1, along)
    sent_upper = lax.slice_in_dim(padded, 0, width, 1, along)
    sent_lower = lax.slice_in_dim(padded, width + extent, 2 * width + extent, 1, along)
    upper = jnp.where(position == 0, upper, sent_upper)
    lower = jnp.where(position == final_index, lower, sent_lower)
    return jnp.concatenate([upper, inside, lower], along)


def rows_apart(field):
    extent = field.shape[1]
    padded = padded_2(field, (("row", 1),), 2)
    padded = reflect_edges(padded, 1, lax.axis_index("row"), lax.axis_size("row") - 1, extent)
    return decimate(padded, 1, extent)


def cols_apart(field):
    extent = field.shape[2]
    padded = padded_2(field, (("col", 2),), 2)
    padded = reflect_edges(padded, 2, lax.axis_index("col"), lax.axis_size("col") - 1, extent)
    return decimate(padded, 2, extent)


def level_sharded(field):
    return cols_apart(rows_apart(field))


def levels_from_margin(padded, margins, height, across):
    row_place = lax.axis_index("row")
    col_place = lax.axis_index("col")
    row_final = lax.axis_size("row") - 1
    col_final = lax.axis_size("col") - 1
    levels = []
    for width in margins:
        padded = reflect_deep(padded, 1, row_place, row_final, height, width)
        padded = reflect_deep(padded, 2, col_place, col_final, across, width)
        height = height // 2
        across = across // 2
        kept = (width - 2) // 2
        padded = decimate_count(padded, 1, height + 2 * kept)
        padded = decimate_count(padded, 2, across + 2 * kept)
        levels.append(padded[:, kept : kept + height, kept : kept + across])
    return levels


def coarse_pair(level_two):
    padded = padded_2(level_two, (("row", 1), ("col", 2)), coarse_margins[0])
    return levels_from_margin(padded, coarse_margins, level_two.shape[1], level_two.shape[2])


def local(relief):
    level_one = level_sharded(relief)
    level_two = level_sharded(level_one)
    level_three, level_four = coarse_pair(level_two)
    return (level_one, level_two, level_three, level_four)


def solution(mesh):
    placed = (P(None, "row", "col"),)
    return jax.shard_map(
        local,
        mesh=mesh,
        in_specs=placed,
        out_specs=(
            P(None, "row", "col"),
            P(None, "row", "col"),
            P(None, "row", "col"),
            P(None, "row", "col"),
        ),
        check_vma=False,
    )
```

profile of v0, /device:TPU:39, one launch (start us, length us, event | category | flops | bytes accessed | tf_op | source)
XLA Modules:
  0.0 342.9 jit_solution(3618606040790743888)
XLA Ops:
  1.7 3.7 %collective-permute-start = (f32[3,2,1024]{2,1,0:T(2,128)S(1)}, f32[3,2,1024]{2,1,0:T(2,128)S(1)}, u32[]{:S(2)}, u32[]{:S(2)}) collective-permute-start(f32[3,2,1024]{2,1,0:T(2,128)S(1)} %get-tuple-element.4), channel_id=1, source_target_pairs={{0,8},{8,16},{16,24},{24,32},{32,40},{40,48},{48,56},{56,64},{64,7... | collective-permute-start | bytes 73736 | tf_op jit(solution)/shard_map/ppermute | solution.py:19
  7.3 7.7 %slice.249 = f32[3,128,1024]{2,1,0:T(8,128)} slice(f32[3,256,1024]{2,1,0:T(8,128)} %param.1), slice={[0:3:1], [0:255:2], [0:1024:1]} | slice | bytes 3145728 | tf_op jit(solution)/shard_map/slice | solution.py:31
  15.1 4.2 %slice.250 = f32[3,128,1024]{2,1,0:T(8,128)} slice(f32[3,256,1024]{2,1,0:T(8,128)S(1)} %copy-done), slice={[0:3:1], [1:256:2], [0:1024:1]} | slice | bytes 3145728 | tf_op jit(solution)/shard_map/slice | solution.py:31
  19.9 2.3 pad_maximum_fusion
  22.2 4.2 %slice.247 = f32[3,128,1024]{2,1,0:T(8,128)} slice(f32[3,260,1024]{2,1,0:T(8,128)S(1)} %pad_maximum_fusion), slice={[0:3:1], [0:255:2], [0:1024:1]} | slice | bytes 3145728 | tf_op jit(solution)/shard_map/slice | solution.py:29
  26.4 4.2 %slice.248 = f32[3,128,1024]{2,1,0:T(8,128)} slice(f32[3,260,1024]{2,1,0:T(8,128)S(1)} %pad_maximum_fusion), slice={[0:3:1], [1:256:2], [0:1024:1]} | slice | bytes 3145728 | tf_op jit(solution)/shard_map/slice | solution.py:31
  30.6 4.3 %slice.251 = f32[3,128,1024]{2,1,0:T(8,128)} slice(f32[3,260,1024]{2,1,0:T(8,128)S(1)} %pad_maximum_fusion), slice={[0:3:1], [4:259:2], [0:1024:1]} | slice | bytes 3145728 | tf_op jit(solution)/shard_map/slice | solution.py:31
  34.9 4.2 %multiply_add_fusion = f32[3,128,1024]{2,1,0:T(8,128)S(1)} fusion(f32[3,128,1024]{2,1,0:T(8,128)} %slice.251, f32[3,128,1024]{2,1,0:T(8,128)} %slice.250, f32[3,128,1024]{2,1,0:T(8,128)} %slice.249, f32[3,128,1024]{2,1,0:T(8,128)} %slice.248, f32[3,128,1024]{2,1,0:T(8,128)} %slice.247), kind=kLoop, calls=%fused_computation.1 | loop fusion | flops 3538944 | bytes 9437184 | tf_op jit(solution)/shard_map/add | solution.py:31
  41.3 35.3 %slice.258 = f32[3,128,512]{2,1,0:T(8,128)} slice(f32[3,128,1024]{2,1,0:T(8,128)S(1)} %multiply_add_fusion), slice={[0:3:1], [0:128:1], [0:1023:2]} | slice | bytes 1572864 | tf_op jit(solution)/shard_map/slice | solution.py:31
  76.6 35.3 %slice.259 = f32[3,128,512]{2,1,0:T(8,128)} slice(f32[3,128,1024]{2,1,0:T(8,128)S(1)} %multiply_add_fusion), slice={[0:3:1], [0:128:1], [1:1024:2]} | slice | bytes 1572864 | tf_op jit(solution)/shard_map/slice | solution.py:31
  112.2 4.0 %collective-permute-start.2 = (f32[3,128,2]{2,1,0:T(8,128)S(1)}, f32[3,128,2]{2,1,0:T(8,128)S(1)}, u32[]{:S(2)}, u32[]{:S(2)}) collective-permute-start(f32[3,128,2]{2,1,0:T(8,128)S(1)} %get-tuple-element.10), channel_id=1, source_target_pairs={{0,1},{1,2},{2,3},{3,4},{4,5},{5,6},{6,7},{8,9},{9,10},{10,11},{11... | collective-permute-start | bytes 9224 | tf_op jit(solution)/shard_map/ppermute | solution.py:19
  116.5 3.3 collective-permute-done.2
  122.4 35.3 %slice.256 = f32[3,128,512]{2,1,0:T(8,128)} slice(f32[3,128,1028]{2,1,0:T(8,128)S(1)} %concatenate.31), slice={[0:3:1], [0:128:1], [0:1023:2]} | slice | bytes 1572864 | tf_op jit(solution)/shard_map/slice | solution.py:29
  157.7 35.3 %slice.257 = f32[3,128,512]{2,1,0:T(8,128)} slice(f32[3,128,1028]{2,1,0:T(8,128)S(1)} %concatenate.31), slice={[0:3:1], [0:128:1], [1:1024:2]} | slice | bytes 1572864 | tf_op jit(solution)/shard_map/slice | solution.py:31
  193.0 35.4 %slice.260 = f32[3,128,512]{2,1,0:T(8,128)} slice(f32[3,128,1028]{2,1,0:T(8,128)S(1)} %concatenate.31), slice={[0:3:1], [0:128:1], [4:1027:2]} | slice | bytes 1572864 | tf_op jit(solution)/shard_map/slice | solution.py:31
  228.4 2.3 multiply_add_fusion.1
  230.7 5.8 %collective-permute-start.4 = (f32[3,2,512]{2,1,0:T(2,128)S(1)}, f32[3,2,512]{2,1,0:T(2,128)S(1)}, u32[]{:S(2)}, u32[]{:S(2)}) collective-permute-start(f32[3,2,512]{2,1,0:T(2,128)S(1)} %get-tuple-element.12), channel_id=1, source_target_pairs={{0,8},{8,16},{16,24},{24,32},{32,40},{40,48},{48,56},{56,64},{64,7... | collective-permute-start | bytes 36872 | tf_op jit(solution)/shard_map/ppermute | solution.py:19
  239.5 5.0 %collective-permute-done.5 = f32[3,2,512]{2,1,0:T(2,128)S(1)} collective-permute-done((f32[3,2,512]{2,1,0:T(2,128)S(1)}, f32[3,2,512]{2,1,0:T(2,128)S(1)}, u32[]{:S(2)}, u32[]{:S(2)}) %collective-permute-start.5) | collective-permute-done | bytes 12320 | tf_op jit(solution)/shard_map/ppermute | solution.py:21
  246.1 3.7 %collective-permute-start.6 = (f32[3,64,2]{2,1,0:T(8,128)S(1)}, f32[3,64,2]{2,1,0:T(8,128)S(1)}, u32[]{:S(2)}, u32[]{:S(2)}) collective-permute-start(f32[3,64,2]{2,1,0:T(8,128)S(1)} %get-tuple-element.20), channel_id=1, source_target_pairs={{0,1},{1,2},{2,3},{3,4},{4,5},{5,6},{6,7},{8,9},{9,10},{10,11},{11... | collective-permute-start | bytes 4616 | tf_op jit(solution)/shard_map/ppermute | solution.py:19
  249.9 8.9 %slice.276 = f32[3,64,256]{2,1,0:T(8,128)S(1)} slice(f32[3,64,512]{2,1,0:T(8,128)S(1)} %multiply_add_fusion.2), slice={[0:3:1], [0:64:1], [0:511:2]} | slice | bytes 393216 | tf_op jit(solution)/shard_map/slice | solution.py:31
  258.8 8.9 %slice.277 = f32[3,64,256]{2,1,0:T(8,128)S(1)} slice(f32[3,64,512]{2,1,0:T(8,128)S(1)} %multiply_add_fusion.2), slice={[0:3:1], [0:64:1], [1:512:2]} | slice | bytes 393216 | tf_op jit(solution)/shard_map/slice | solution.py:31
  267.7 2.1 collective-permute-start.7
  270.0 3.9 %collective-permute-done.7 = f32[3,64,2]{2,1,0:T(8,128)S(1)} collective-permute-done((f32[3,64,2]{2,1,0:T(8,128)S(1)}, f32[3,64,2]{2,1,0:T(8,128)S(1)}, u32[]{:S(2)}, u32[]{:S(2)}) %collective-permute-start.7) | collective-permute-done | bytes 1568 | tf_op jit(solution)/shard_map/ppermute | solution.py:21
  274.2 8.9 %slice.274 = f32[3,64,256]{2,1,0:T(8,128)S(1)} slice(f32[3,64,516]{2,1,0:T(8,128)S(1)} %pad_maximum_fusion.2), slice={[0:3:1], [0:64:1], [0:511:2]} | slice | bytes 393216 | tf_op jit(solution)/shard_map/slice | solution.py:29
  283.1 8.9 %slice.275 = f32[3,64,256]{2,1,0:T(8,128)S(1)} slice(f32[3,64,516]{2,1,0:T(8,128)S(1)} %pad_maximum_fusion.2), slice={[0:3:1], [0:64:1], [1:512:2]} | slice | bytes 393216 | tf_op jit(solution)/shard_map/slice | solution.py:31
  292.0 8.9 %slice.278 = f32[3,64,256]{2,1,0:T(8,128)S(1)} slice(f32[3,64,516]{2,1,0:T(8,128)S(1)} %pad_maximum_fusion.2), slice={[0:3:1], [0:64:1], [4:515:2]} | slice | bytes 393216 | tf_op jit(solution)/shard_map/slice | solution.py:31
  301.0 3.1 collective-permute-start.8
  306.0 5.3 %collective-permute-done.9 = f32[3,6,256]{2,1,0:T(8,128)S(1)} collective-permute-done((f32[3,6,256]{2,1,0:T(8,128)S(1)}, f32[3,6,256]{2,1,0:T(8,128)S(1)}, u32[]{:S(2)}, u32[]{:S(2)}) %collective-permute-start.9) | collective-permute-done | bytes 18464 | tf_op jit(solution)/shard_map/ppermute | solution.py:21
  311.5 5.3 %collective-permute-start.10 = (f32[3,76,6]{2,1,0:T(8,128)S(1)}, f32[3,76,6]{2,1,0:T(8,128)S(1)}, u32[]{:S(2)}, u32[]{:S(2)}) collective-permute-start(f32[3,76,6]{2,1,0:T(8,128)S(1)} %get-tuple-element.28), channel_id=1, source_target_pairs={{0,1},{1,2},{2,3},{3,4},{4,5},{5,6},{6,7},{8,9},{9,10},{10,11},{11... | collective-permute-start | bytes 16424 | tf_op jit(solution)/shard_map/ppermute | solution.py:19
  318.8 5.2 %collective-permute-done.11 = f32[3,76,6]{2,1,0:T(8,128)S(1)} collective-permute-done((f32[3,76,6]{2,1,0:T(8,128)S(1)}, f32[3,76,6]{2,1,0:T(8,128)S(1)}, u32[]{:S(2)}, u32[]{:S(2)}) %collective-permute-start.11) | collective-permute-done | bytes 5504 | tf_op jit(solution)/shard_map/ppermute | solution.py:21
  331.5 2.0 slice.300
  335.6 2.0 slice.302
  (101 shorter events, 32.0 us)
Async XLA Ops:
  1.7 18.1 %collective-permute-start = (f32[3,2,1024]{2,1,0:T(2,128)S(1)}, f32[3,2,1024]{2,1,0:T(2,128)S(1)}, u32[]{:S(2)}, u32[]{:S(2)}) collective-permute-start(f32[3,2,1024]{2,1,0:T(2,128)S(1)} %get-tuple-element.4), channel_id=1, source_target_pairs={{0,8},{8,16},{16,24},{24,32},{32,40},{40,48},{48,56},{56,64},{64,7... | collective-permute-start | bytes 73736 | tf_op jit(solution)/shard_map/ppermute | solution.py:19
  5.4 14.5 %collective-permute-start.1 = (f32[3,2,1024]{2,1,0:T(2,128)S(1)}, f32[3,2,1024]{2,1,0:T(2,128)S(1)}, u32[]{:S(2)}, u32[]{:S(2)}) collective-permute-start(f32[3,2,1024]{2,1,0:T(2,128)S(1)} %get-tuple-element.5), channel_id=1, source_target_pairs={{8,0},{16,8},{24,16},{32,24},{40,32},{48,40},{56,48},{64,56},{72,6... | collective-permute-start | bytes 73736 | tf_op jit(solution)/shard_map/ppermute | solution.py:21
  7.3 7.8 %copy-start = (f32[3,256,1024]{2,1,0:T(8,128)S(1)}, f32[3,256,1024]{2,1,0:T(8,128)}, u32[]{:S(2)}) copy-start(f32[3,256,1024]{2,1,0:T(8,128)} %param.1) | copy-start | bytes 9437188
  39.3 77.1 %collective-permute-start.3 = (f32[3,128,2]{2,1,0:T(8,128)S(1)}, f32[3,128,2]{2,1,0:T(8,128)S(1)}, u32[]{:S(2)}, u32[]{:S(2)}) collective-permute-start(f32[3,128,2]{2,1,0:T(8,128)S(1)} %get-tuple-element.8), channel_id=1, source_target_pairs={{1,0},{2,1},{3,2},{4,3},{5,4},{6,5},{7,6},{9,8},{10,9},{11,10},{12... | collective-permute-start | bytes 9224 | tf_op jit(solution)/shard_map/ppermute | solution.py:21
  112.2 7.6 %collective-permute-start.2 = (f32[3,128,2]{2,1,0:T(8,128)S(1)}, f32[3,128,2]{2,1,0:T(8,128)S(1)}, u32[]{:S(2)}, u32[]{:S(2)}) collective-permute-start(f32[3,128,2]{2,1,0:T(8,128)S(1)} %get-tuple-element.10), channel_id=1, source_target_pairs={{0,1},{1,2},{2,3},{3,4},{4,5},{5,6},{6,7},{8,9},{9,10},{10,11},{11... | collective-permute-start | bytes 9224 | tf_op jit(solution)/shard_map/ppermute | solution.py:19
  157.7 70.7 %copy-start.3 = (f32[3,128,512]{2,1,0:T(8,128)S(1)}, f32[3,128,512]{2,1,0:T(8,128)}, u32[]{:S(2)}) copy-start(f32[3,128,512]{2,1,0:T(8,128)} %slice.258) | copy-start | bytes 2359300
  230.7 14.0 %copy-start.1 = (f32[3,128,512]{2,1,0:T(8,128)}, f32[3,128,512]{2,1,0:T(8,128)S(1)}, u32[]{:S(2)}) copy-start(f32[3,128,512]{2,1,0:T(8,128)S(1)} %multiply_add_fusion.1) | copy-start | bytes 2359300
  230.7 8.8 %collective-permute-start.4 = (f32[3,2,512]{2,1,0:T(2,128)S(1)}, f32[3,2,512]{2,1,0:T(2,128)S(1)}, u32[]{:S(2)}, u32[]{:S(2)}) collective-permute-start(f32[3,2,512]{2,1,0:T(2,128)S(1)} %get-tuple-element.12), channel_id=1, source_target_pairs={{0,8},{8,16},{16,24},{24,32},{32,40},{40,48},{48,56},{56,64},{64,7... | collective-permute-start | bytes 36872 | tf_op jit(solution)/shard_map/ppermute | solution.py:19
  237.4 7.1 %collective-permute-start.5 = (f32[3,2,512]{2,1,0:T(2,128)S(1)}, f32[3,2,512]{2,1,0:T(2,128)S(1)}, u32[]{:S(2)}, u32[]{:S(2)}) collective-permute-start(f32[3,2,512]{2,1,0:T(2,128)S(1)} %get-tuple-element.13), channel_id=1, source_target_pairs={{8,0},{16,8},{24,16},{32,24},{40,32},{48,40},{56,48},{64,56},{72,6... | collective-permute-start | bytes 36872 | tf_op jit(solution)/shard_map/ppermute | solution.py:21
  246.1 23.8 %collective-permute-start.6 = (f32[3,64,2]{2,1,0:T(8,128)S(1)}, f32[3,64,2]{2,1,0:T(8,128)S(1)}, u32[]{:S(2)}, u32[]{:S(2)}) collective-permute-start(f32[3,64,2]{2,1,0:T(8,128)S(1)} %get-tuple-element.20), channel_id=1, source_target_pairs={{0,1},{1,2},{2,3},{3,4},{4,5},{5,6},{6,7},{8,9},{9,10},{10,11},{11... | collective-permute-start | bytes 4616 | tf_op jit(solution)/shard_map/ppermute | solution.py:19
  267.7 6.2 %collective-permute-start.7 = (f32[3,64,2]{2,1,0:T(8,128)S(1)}, f32[3,64,2]{2,1,0:T(8,128)S(1)}, u32[]{:S(2)}, u32[]{:S(2)}) collective-permute-start(f32[3,64,2]{2,1,0:T(8,128)S(1)} %get-tuple-element.21), channel_id=1, source_target_pairs={{1,0},{2,1},{3,2},{4,3},{5,4},{6,5},{7,6},{9,8},{10,9},{11,10},{12... | collective-permute-start | bytes 4616 | tf_op jit(solution)/shard_map/ppermute | solution.py:21
  301.0 23.8 %copy-start.2 = (f32[3,64,256]{2,1,0:T(8,128)}, f32[3,64,256]{2,1,0:T(8,128)S(1)}, u32[]{:S(2)}) copy-start(f32[3,64,256]{2,1,0:T(8,128)S(1)} %multiply_add_fusion.3) | copy-start | bytes 589828
  301.0 5.0 %collective-permute-start.8 = (f32[3,6,256]{2,1,0:T(8,128)S(1)}, f32[3,6,256]{2,1,0:T(8,128)S(1)}, u32[]{:S(2)}, u32[]{:S(2)}) collective-permute-start(f32[3,6,256]{2,1,0:T(8,128)S(1)} %get-tuple-element.30), channel_id=1, source_target_pairs={{0,8},{8,16},{16,24},{24,32},{32,40},{40,48},{48,56},{56,64},{64,7... | collective-permute-start | bytes 55304 | tf_op jit(solution)/shard_map/ppermute | solution.py:19
  304.1 7.3 %collective-permute-start.9 = (f32[3,6,256]{2,1,0:T(8,128)S(1)}, f32[3,6,256]{2,1,0:T(8,128)S(1)}, u32[]{:S(2)}, u32[]{:S(2)}) collective-permute-start(f32[3,6,256]{2,1,0:T(8,128)S(1)} %get-tuple-element.31), channel_id=1, source_target_pairs={{8,0},{16,8},{24,16},{32,24},{40,32},{48,40},{56,48},{64,56},{72,6... | collective-permute-start | bytes 55304 | tf_op jit(solution)/shard_map/ppermute | solution.py:21
  311.5 7.3 %collective-permute-start.10 = (f32[3,76,6]{2,1,0:T(8,128)S(1)}, f32[3,76,6]{2,1,0:T(8,128)S(1)}, u32[]{:S(2)}, u32[]{:S(2)}) collective-permute-start(f32[3,76,6]{2,1,0:T(8,128)S(1)} %get-tuple-element.28), channel_id=1, source_target_pairs={{0,1},{1,2},{2,3},{3,4},{4,5},{5,6},{6,7},{8,9},{9,10},{10,11},{11... | collective-permute-start | bytes 16424 | tf_op jit(solution)/shard_map/ppermute | solution.py:19
  316.8 7.1 %collective-permute-start.11 = (f32[3,76,6]{2,1,0:T(8,128)S(1)}, f32[3,76,6]{2,1,0:T(8,128)S(1)}, u32[]{:S(2)}, u32[]{:S(2)}) collective-permute-start(f32[3,76,6]{2,1,0:T(8,128)S(1)} %get-tuple-element.29), channel_id=1, source_target_pairs={{1,0},{2,1},{3,2},{4,3},{5,4},{6,5},{7,6},{9,8},{10,9},{11,10},{12... | collective-permute-start | bytes 16424 | tf_op jit(solution)/shard_map/ppermute | solution.py:21
where the time goes:
time: 349 us; the launch traced here: 343 us
  local copies, waits for them, and re-layouts  269 us (77%)
  starting transfers between devices  37.3 us (11%)
  waiting for transfers between devices  22.7 us (7%)
  other arithmetic  12.1 us (3%)
    slice x16, local copies, waits for them, and re-layouts, decimate(): lax.slice_in_dim(padded, offset, offset + extent - 1, 2, along)  199 us
    slice x4, local copies, waits for them, and re-layouts, decimate(): result = binomial[0] * lax.slice_in_dim(padded, 0, extent - 1, 2, along)  48.7 us
    ppermute x6, starting transfers between devices, padded_2(): lax.ppermute(tail, axis, [(i, (i + 1) % count) for i in range(ends)])  25.6 us
    ppermute x6, waiting for transfers between devices, padded_2(): lax.ppermute(head, axis, [((i + 1) % count, i) for i in range(ends)])  19.4 us
    ppermute x6, starting transfers between devices, padded_2(): lax.ppermute(head, axis, [((i + 1) % count, i) for i in range(ends)])  11.7 us
    slice x16, local copies, waits for them, and re-layouts, decimate_count(): lax.slice_in_dim(padded, offset, offset + 2 * count - 1, 2, along)  11.2 us
  transfers between devices with their start and end apart: 12, of which 5 were waited for; matrix products, arithmetic and copies ran while one was open for 30% of the time, Pallas kernels for 0%

commit v1 on v0

v1 whole, which is shorter than its diff:
```python
import functools

import jax
import jax.numpy as jnp
import numpy as np
from jax import lax
from jax.experimental import pallas as pl
from jax.experimental.pallas import tpu as pltpu
from jax.sharding import PartitionSpec as P

MESH = pl.DeviceIdType.MESH
BINOMIAL = np.array([1, 4, 6, 4, 1]) / 16
LEVELS = 4
PAD = 8
ROW_STRIP = 32
COL_STRIP = 128
HIGHEST = lax.Precision.HIGHEST


def reduce_matrix(n, reflect):
    d = np.zeros((n // 2, n))
    for i in range(n // 2):
        for t in range(5):
            c = 2 * i - 2 + t
            if c < 0 or c >= n:
                if not reflect:
                    continue
                c = -c if c < 0 else 2 * (n - 1) - c
            d[i, c] += BINOMIAL[t]
    return d


def chain(n, reflect):
    out, m = [], np.eye(n)
    for _ in range(LEVELS):
        m = reduce_matrix(m.shape[0], reflect) @ m
        out.append(m)
    return out


def edge_parts(n):
    whole, alone = chain(3 * n, True), chain(n, False)
    places = []
    for p in range(3):
        parts = []
        for k in range(LEVELS):
            m = n >> (k + 1)
            mine = whole[k][:, p * n : (p + 1) * n]
            own = mine[p * m : (p + 1) * m] - alone[k]
            assert not own[2:-1].any()
            up = mine[(p + 1) * m : (p + 1) * m + 2] if p < 2 else np.zeros((2, n))
            down = mine[p * m - 1 : p * m] if p > 0 else np.zeros((1, n))
            parts.append((up, down, own[:2], own[-1:]))
        places.append(parts)
    return places


def ends(rows, strip):
    return np.concatenate([rows[:, :strip], rows[:, -strip:]], 1)


def tables():
    places = edge_parts(256)
    row_table = np.zeros((3, 32, 2 * ROW_STRIP), np.float32)
    col_table = np.zeros((3, 24 * LEVELS, 2 * COL_STRIP), np.float32)
    for p, parts in enumerate(places):
        for k, (up, down, first, last) in enumerate(parts):
            row_table[p, 2 * k : 2 * k + 2] = ends(up, ROW_STRIP)
            row_table[p, 8 + k] = ends(down, ROW_STRIP)[0]
            row_table[p, 16 + 2 * k : 18 + 2 * k] = ends(first, ROW_STRIP)
            row_table[p, 24 + k] = ends(last, ROW_STRIP)[0]
            col_table[p, 24 * k : 24 * k + 2] = ends(up, COL_STRIP)
            col_table[p, 24 * k + 15] = ends(down, COL_STRIP)[0]
            col_table[p, 24 * k + 16 : 24 * k + 18] = ends(first, COL_STRIP)
            col_table[p, 24 * k + 23] = ends(last, COL_STRIP)[0]
    return row_table, col_table


def split(a):
    high = a.astype(jnp.bfloat16)
    return high, (a - high.astype(jnp.float32)).astype(jnp.bfloat16)


def dot_split(a, weights):
    high, low = split(a)
    dot = functools.partial(jnp.dot, preferred_element_type=jnp.float32)
    return dot(high, weights) + dot(low, weights)


def place(index, count):
    return jnp.where(index == 0, 0, jnp.where(index == count - 1, 2, 1))


def pyramid_kernel(
    rows_n, cols_n, x_hbm, rt_hbm, ct_hbm, c1_hbm, c12_hbm, c3_hbm, c4_hbm,
    o1, o2, o3, o4,
    x, y1, y2, y3, y4, rt, ct, c1, c12, c3, c4,
    zsend_up, zsend_down, zown, zfrom_low, zfrom_high,
    vsend_up, vsend_down, vown, vfrom_low, vfrom_high,
    x_sem, t_sem, z_sem, v_sem,
):
    bands, height, width = x_hbm.shape
    r, c = lax.axis_index("row"), lax.axis_index("col")
    has_low_row, has_high_row = r > 0, r < rows_n - 1
    has_low_col, has_high_col = c > 0, c < cols_n - 1
    ys = (y1, y2, y3, y4)
    fields = (x,) + ys

    barrier = pltpu.get_barrier_semaphore()
    for axis, has, step in (
        ("row", has_low_row, -1), ("row", has_high_row, 1), ("col", has_low_col, -1), ("col", has_high_col, 1)
    ):

        @pl.when(has)
        def _(axis=axis, step=step):
            pl.semaphore_signal(
                barrier, inc=1, device_id={axis: lax.axis_index(axis) + step}, device_id_type=MESH
            )

    def load(source, target, sem):
        copy = pltpu.make_async_copy(source, target, sem)
        copy.start()
        return copy

    row_copy = load(rt_hbm.at[place(r, rows_n)], rt, t_sem.at[0])
    tiles = width // 128

    def load_rows(b, begin, end, sem):
        return [
            load(
                x_hbm.at[b, begin:end, 128 * i : 128 * i + 128],
                x.at[b, i, PAD + begin : PAD + end],
                sem.at[i],
            )
            for i in range(tiles)
        ]

    strips = [
        load_rows(b, 0, ROW_STRIP, x_sem.at[0, b])
        + load_rows(b, height - ROW_STRIP, height, x_sem.at[1, b])
        for b in range(bands)
    ]
    middles = [load_rows(b, ROW_STRIP, height - ROW_STRIP, x_sem.at[2, b]) for b in range(bands)]
    rest = [
        load(ct_hbm.at[place(c, cols_n)], ct, t_sem.at[1]),
        load(c1_hbm, c1, t_sem.at[2]),
        load(c12_hbm, c12, t_sem.at[3]),
        load(c3_hbm, c3, t_sem.at[4]),
        load(c4_hbm, c4, t_sem.at[5]),
    ]

    for field in fields[:LEVELS]:
        size = field.shape[2] - 2 * PAD
        zeros = jnp.zeros((bands, tiles, PAD, 128), jnp.float32)
        field[:, :, 0:PAD] = zeros
        field[:, :, PAD + size :] = zeros

    def across(field, b, begin, end, lanes=range(tiles)):
        return jnp.concatenate([field[b, i, PAD + begin : PAD + end] for i in lanes], 1)

    row_copy.wait()
    for b in range(bands):
        for copy in strips[b]:
            copy.wait()
        strip = jnp.concatenate(
            [across(x, b, 0, ROW_STRIP), across(x, b, height - ROW_STRIP, height)], 0
        )
        z = jnp.dot(rt[...], strip, precision=HIGHEST, preferred_element_type=jnp.float32)
        zsend_up[b] = z[0:8]
        zsend_down[b] = z[8:16]
        zown[b] = z[16:32]

    neighbours = (
        has_low_row.astype(jnp.int32)
        + has_high_row.astype(jnp.int32)
        + has_low_col.astype(jnp.int32)
        + has_high_col.astype(jnp.int32)
    )
    pl.semaphore_wait(barrier, neighbours)

    def exchange(axis, has_low, has_high, up, down, from_low, from_high, sem):
        here = lax.axis_index(axis)
        to_high = pltpu.make_async_remote_copy(
            up, from_low, sem.at[0], sem.at[1], device_id={axis: here + 1}, device_id_type=MESH
        )
        to_low = pltpu.make_async_remote_copy(
            down, from_high, sem.at[2], sem.at[3], device_id={axis: here - 1}, device_id_type=MESH
        )
        pl.when(has_high)(to_high.start)
        pl.when(has_low)(to_low.start)

        def arrive():
            pl.when(has_low)(to_high.wait_recv)
            pl.when(has_high)(to_low.wait_recv)

        def sent():
            pl.when(has_high)(to_high.wait_send)
            pl.when(has_low)(to_low.wait_send)

        return arrive, sent

    z_arrive, z_sent = exchange(
        "row", has_low_row, has_high_row, zsend_up, zsend_down, zfrom_low, zfrom_high, z_sem
    )

    for b in range(bands):
        for copy in middles[b]:
            copy.wait()

        def reduce_tile(i, carry, b=b):
            for source, target in zip(fields[:LEVELS], ys):
                size = target.shape[2] - 2 * PAD
                tap = [source[b, i, pl.ds(PAD - 2 + t, size, stride=2)] for t in range(5)]
                target[b, i, PAD : PAD + size] = (
                    0.0625 * (tap[0] + tap[4]) + 0.25 * (tap[1] + tap[3]) + 0.375 * tap[2]
                )
            return carry

        lax.fori_loop(0, tiles, reduce_tile, 0)

    z_arrive()
    for b in range(bands):
        first = jnp.where(has_low_row, zfrom_low[b], 0.0) + zown[b, 0:8]
        last = jnp.where(has_high_row, zfrom_high[b], 0.0) + zown[b, 8:16]
        for k, y in enumerate(ys):
            size = y.shape[2] - 2 * PAD
            for i in range(tiles):
                lanes = slice(128 * i, 128 * i + 128)
                y[b, i, PAD : PAD + 2] = y[b, i, PAD : PAD + 2] + first[2 * k : 2 * k + 2, lanes]
                end = slice(PAD + size - 1, PAD + size)
                y[b, i, end] = y[b, i, end] + last[k : k + 1, lanes]

    def rows_of(b, levels, lanes=range(tiles)):
        return jnp.concatenate([across(ys[k], b, 0, height >> (k + 1), lanes) for k in levels], 0)

    for copy in rest:
        copy.wait()
    lane = lax.broadcasted_iota(jnp.int32, (24, height), 1)
    for b in range(bands):
        edge = rows_of(b, range(LEVELS), (0, tiles - 1))
        edge = jnp.concatenate([edge, jnp.zeros((height >> LEVELS, 2 * COL_STRIP), jnp.float32)], 0)
        v = lax.dot_general(
            ct[...], edge, (((1,), (1,)), ((), ())), precision=HIGHEST, preferred_element_type=jnp.float32
        )
        picked = v[72:96]
        for k in range(LEVELS - 2, -1, -1):
            picked = jnp.where(lane < height - (height >> (k + 1)), v[24 * k : 24 * k + 24], picked)
        vsend_up[b] = picked[0:8]
        vsend_down[b] = picked[8:16]
        vown[b] = picked[16:24]
    v_arrive, v_sent = exchange(
        "col", has_low_col, has_high_col, vsend_up, vsend_down, vfrom_low, vfrom_high, v_sem
    )

    half = width // 2
    for b in range(bands):
        high, low = split(rows_of(b, (0,)))
        dot = functools.partial(jnp.dot, preferred_element_type=jnp.float32)
        o1[b, :, 0 : half // 2] = dot(high[:, : half + 128], c1[0]) + dot(low[:, : half + 128], c1[0])
        o1[b, :, half // 2 :] = dot(high[:, half - 128 :], c1[1]) + dot(low[:, half - 128 :], c1[1])
        two = dot_split(rows_of(b, range(1, LEVELS)), c12[...])
        o2[b] = two[: height // 4]
        three = dot_split(two[height // 4 :], c3[...])
        o3[b] = three[: height // 8]
        o4[b] = dot_split(three[height // 8 :], c4[...])[:, : width >> 4]

    v_arrive()
    at = lax.broadcasted_iota(jnp.int32, (128, 128), 1)
    for b in range(bands):
        edge = (
            jnp.where(has_low_col, vfrom_low[b], 0.0)
            + jnp.where(has_high_col, vfrom_high[b], 0.0)
            + vown[b]
        )
        for part, levels in ((0, (0,)), (1, (1, 2, 3))):
            square = jnp.concatenate(
                [edge[:, 128 * part : 128 * part + 128], jnp.zeros((120, 128), jnp.float32)], 0
            ).T
            start = 0
            for k in levels:
                out = (o1, o2, o3, o4)[k]
                size, across = out.shape[1:]
                cells = square[start : start + size]
                start += size
                tile = min(across, 128)
                first = jnp.where(at[:size] < 2, cells, 0.0)[:, :tile]
                last = jnp.where(at[:size] == tile - 1, pltpu.roll(cells, tile - 8, 1), 0.0)[:, :tile]
                out[b, :, 0:tile] = out[b, :, 0:tile] + first
                out[b, :, across - tile :] = out[b, :, across - tile :] + last
    z_sent()
    v_sent()


def store_kernel(*refs):
    sources, targets, sem = refs[:LEVELS], refs[LEVELS : 2 * LEVELS], refs[2 * LEVELS]
    copies = [pltpu.make_async_copy(s, t, sem.at[k]) for k, (s, t) in enumerate(zip(sources, targets))]
    for copy in copies:
        copy.start()
    for copy in copies:
        copy.wait()


def solution(mesh):
    rows_n, cols_n = mesh.shape["row"], mesh.shape["col"]
    row_table, col_table = tables()

    def local(relief):
        bands, height, width = relief.shape
        f32, bf16 = jnp.float32, jnp.bfloat16
        half = width // 2
        one = reduce_matrix(width, False).T
        c1 = np.stack([one[: half + 128, : half // 2], one[half - 128 :, half // 2 :]])
        c12 = chain(width, False)[1].T
        c3 = reduce_matrix(width // 4, False).T
        c4 = np.zeros((width // 8, 128))
        c4[:, : width // 16] = reduce_matrix(width // 8, False).T
        consts = [jnp.asarray(row_table), jnp.asarray(col_table)]
        consts += [jnp.asarray(a, bf16) for a in (c1, c12, c3, c4)]
        shapes = [(bands, height >> k, width >> k) for k in range(1, LEVELS + 1)]

        vmem = lambda *shape, dtype=f32: pltpu.VMEM(shape, dtype)
        scratch = [vmem(bands, width // 128, (height >> k) + 2 * PAD, 128) for k in range(LEVELS + 1)]
        scratch += [
            vmem(*row_table.shape[1:]), vmem(*col_table.shape[1:]),
            vmem(*c1.shape, dtype=bf16), vmem(*c12.shape, dtype=bf16),
            vmem(*c3.shape, dtype=bf16), vmem(*c4.shape, dtype=bf16),
            vmem(bands, 8, width), vmem(bands, 8, width), vmem(bands, 16, width),
            vmem(bands, 8, width), vmem(bands, 8, width),
            vmem(bands, 8, height), vmem(bands, 8, height), vmem(bands, 8, height),
            vmem(bands, 8, height), vmem(bands, 8, height),
            pltpu.SemaphoreType.DMA((3, bands, width // 128)), pltpu.SemaphoreType.DMA((6,)),
            pltpu.SemaphoreType.DMA((4,)), pltpu.SemaphoreType.DMA((4,)),
        ]
        held = pl.pallas_call(
            functools.partial(pyramid_kernel, rows_n, cols_n),
            out_shape=[jax.ShapeDtypeStruct(s, f32) for s in shapes],
            in_specs=[pl.BlockSpec(memory_space=pltpu.HBM)] * 7,
            out_specs=[pl.BlockSpec(memory_space=pltpu.VMEM)] * LEVELS,
            scratch_shapes=scratch,
            compiler_params=pltpu.CompilerParams(
                collective_id=0, has_side_effects=True, vmem_limit_bytes=40 << 20
            ),
            name="pyramid",
        )(*[pltpu.with_memory_space_constraint(a, pltpu.HBM) for a in (relief, *consts)])
        return pl.pallas_call(
            store_kernel,
            out_shape=[jax.ShapeDtypeStruct(s, f32) for s in shapes],
            in_specs=[pl.BlockSpec(memory_space=pltpu.VMEM)] * LEVELS,
            out_specs=[pl.BlockSpec(memory_space=pltpu.HBM)] * LEVELS,
            scratch_shapes=[pltpu.SemaphoreType.DMA((LEVELS,))],
            compiler_params=pltpu.CompilerParams(vmem_limit_bytes=16 << 20),
            name="store",
        )(*held)

    spec = P(None, "row", "col")
    return jax.shard_map(local, mesh=mesh, in_specs=(spec,), out_specs=(spec,) * LEVELS, check_vma=False)
```

time: 349 us -> 16.1 us (0.05)
  the two profiles are of different devices: /device:TPU:39 before, /device:TPU:120 now
where the time goes in v1:
time: 16.1 us; the launch traced here: 16 us
  Pallas kernels  15.3 us (95%)
  between operations  0.64 us (4%)
    pallas_call x1, Pallas kernels, local(): pl.pallas_call(functools.partial(pyramid_kernel, rows_n, cols_n), out_sha...  14.4 us
    pallas_call x1, Pallas kernels, local(): pl.pallas_call(store_kernel, out_shape=[jax.ShapeDtypeStruct(s, f32) for...  0.99 us

profile of v1, /device:TPU:120, one launch (start us, length us, event | category | flops | bytes accessed | tf_op | source)
XLA Modules:
  0.0 16.0 jit_solution(17970469197486545864)
XLA Ops:
  0.6 14.4 %pyramid.1 = (f32[3,128,512]{2,1,0:T(8,128)S(1)}, f32[3,64,256]{2,1,0:T(8,128)S(1)}, f32[3,32,128]{2,1,0:T(8,128)S(1)}, f32[3,16,64]{2,1,0:T(8,128)S(1)}) custom-call(f32[3,256,1024]{2,1,0:T(8,128)} %x_hbm.1, f32[3,32,64]{2,1,0:T(8,128)} %constant.12.clone.rt_hbm, f32[3,96,256]{2,1,0:T(8,128)} %constant.13.clone.ct_hbm, ...), custom_call_target="tpu_custom_call" | custom-call | tf_op jit(solution)/shard_map/pyramid/pallas_call | solution.py:334
  15.0 1.0 %store.1 = (f32[3,128,512]{2,1,0:T(8,128)}, f32[3,64,256]{2,1,0:T(8,128)}, f32[3,32,128]{2,1,0:T(8,128)}, f32[3,16,64]{2,1,0:T(8,128)}) custom-call(f32[3,128,512]{2,1,0:T(8,128)S(1)} %get-tuple-element.8.refs_0_, f32[3,64,256]{2,1,0:T(8,128)S(1)} %get-tuple-element.9.refs_1_, f32[3,32,128]{2,1,0:T(8,128)S(1)} %get-tuple-element.10.refs_2_, ...), custom_call_target="tpu_custom_call" | custom-call | tf_op jit(solution)/shard_map/store/pallas_call | solution.py:345

commit v2 on v1

v2 whole, which is shorter than its diff:
```python
import functools

import jax
import jax.numpy as jnp
import numpy as np
from jax import lax
from jax.experimental import pallas as pl
from jax.experimental.pallas import tpu as pltpu
from jax.sharding import PartitionSpec as P

MESH = pl.DeviceIdType.MESH
BINOMIAL = np.array([1, 4, 6, 4, 1]) / 16
LEVELS = 4
PAD = 8
ROW_STRIP = 32
COL_STRIP = 64
UNROLL = 4


def reduce_matrix(n, reflect):
    d = np.zeros((n // 2, n))
    for i in range(n // 2):
        for t in range(5):
            c = 2 * i - 2 + t
            if c < 0 or c >= n:
                if not reflect:
                    continue
                c = -c if c < 0 else 2 * (n - 1) - c
            d[i, c] += BINOMIAL[t]
    return d


def chain(n, reflect):
    out, m = [], np.eye(n)
    for _ in range(LEVELS):
        m = reduce_matrix(m.shape[0], reflect) @ m
        out.append(m)
    return out


def edge_parts(n):
    whole, alone = chain(3 * n, True), chain(n, False)
    places = []
    for p in range(3):
        parts = []
        for k in range(LEVELS):
            m = n >> (k + 1)
            mine = whole[k][:, p * n : (p + 1) * n]
            own = mine[p * m : (p + 1) * m] - alone[k]
            assert not own[2:-1].any()
            up = mine[(p + 1) * m : (p + 1) * m + 2] if p < 2 else np.zeros((2, n))
            down = mine[p * m - 1 : p * m] if p > 0 else np.zeros((1, n))
            parts.append((up, down, own[:2], own[-1:]))
        places.append(parts)
    return places


def ends(rows, strip):
    return np.concatenate([rows[:, :strip], rows[:, -strip:]], 1)


def parts_of(table):
    high = np.asarray(jnp.asarray(table, jnp.bfloat16), np.float32)
    return high, table - high


def tables():
    places = edge_parts(256)
    row_table = np.zeros((3, 32, 2 * ROW_STRIP), np.float32)
    col_table = np.zeros((3, 8 * LEVELS, 2 * COL_STRIP), np.float32)
    for p, parts in enumerate(places):
        for k, (up, down, first, last) in enumerate(parts):
            row_table[p, 2 * k : 2 * k + 2] = ends(up, ROW_STRIP)
            row_table[p, 8 + k] = ends(down, ROW_STRIP)[0]
            row_table[p, 16 + 2 * k : 18 + 2 * k] = ends(first, ROW_STRIP)
            row_table[p, 24 + k] = ends(last, ROW_STRIP)[0]
            col_table[p, 8 * k : 8 * k + 6] = ends(np.concatenate([up, first, last, down]), COL_STRIP)
    high, low = parts_of(row_table)
    row_table = np.concatenate([high, high, low], 2)
    high, low = parts_of(col_table)
    none = np.zeros_like(low)
    col_table = np.concatenate(
        [np.concatenate([high, high], 2), np.concatenate([low, none], 2)], 1
    )
    return row_table, col_table


def split(a):
    high = a.astype(jnp.bfloat16)
    return high, (a - high.astype(jnp.float32)).astype(jnp.bfloat16)


dot = functools.partial(jnp.dot, preferred_element_type=jnp.float32)


def dot_split(a, weights):
    high, low = split(a)
    return dot(high, weights) + dot(low, weights)


def place(index, count):
    return jnp.where(index == 0, 0, jnp.where(index == count - 1, 2, 1))


def pyramid_kernel(
    rows_n, cols_n, x_hbm, rt_hbm, ct_hbm, c1_hbm, c12_hbm, c3_hbm, c4_hbm,
    o1, o2, o3, o4,
    strip, x, y1, y2, y3, y4, s1, s234, edge, rt, ct, c1, c12, c3, c4,
    zsend_up, zsend_down, zown, zfrom_low, zfrom_high,
    esend_up, esend_down, efrom_low, efrom_high,
    vsend, vfrom_low, vfrom_high,
    s_sem, x_sem, t_sem, e_sem, z_sem, v_sem,
):
    bands, height, width = x_hbm.shape
    tiles = width // 128
    r, c = lax.axis_index("row"), lax.axis_index("col")
    has_low_row, has_high_row = r > 0, r < rows_n - 1
    has_low_col, has_high_col = c > 0, c < cols_n - 1
    ys = (y1, y2, y3, y4)
    fields = (x,) + ys
    sizes = [height >> (k + 1) for k in range(LEVELS)]
    starts = [height - (height >> k) for k in range(LEVELS)]

    barrier = pltpu.get_barrier_semaphore()
    for axis, has, step in (
        ("row", has_low_row, -1), ("row", has_high_row, 1), ("col", has_low_col, -1), ("col", has_high_col, 1)
    ):

        @pl.when(has)
        def _(axis=axis, step=step):
            pl.semaphore_signal(
                barrier, inc=1, device_id={axis: lax.axis_index(axis) + step}, device_id_type=MESH
            )

    def load(source, target, sem):
        copy = pltpu.make_async_copy(source, target, sem)
        copy.start()
        return copy

    first_loads = [load(rt_hbm.at[place(r, rows_n)], rt, t_sem.at[0])]
    for b in range(bands):
        for e, begin in enumerate((0, height - ROW_STRIP)):
            first_loads.append(
                load(
                    x_hbm.at[b, begin : begin + ROW_STRIP],
                    strip.at[b, e * ROW_STRIP : (e + 1) * ROW_STRIP],
                    s_sem.at[e, b],
                )
            )
    band_loads = [
        [
            load(x_hbm.at[b, :, 128 * i : 128 * i + 128], x.at[b, i, PAD : PAD + height], x_sem.at[b, i])
            for i in range(tiles)
        ]
        for b in range(bands)
    ]
    rest = [
        load(ct_hbm.at[place(c, cols_n)], ct, t_sem.at[1]),
        load(c1_hbm, c1, t_sem.at[2]),
        load(c12_hbm, c12, t_sem.at[3]),
        load(c3_hbm, c3, t_sem.at[4]),
        load(c4_hbm, c4, t_sem.at[5]),
    ]

    for field in fields[:LEVELS]:
        size = field.shape[2] - 2 * PAD
        zeros = jnp.zeros((bands, tiles, PAD, 128), jnp.float32)
        field[:, :, 0:PAD] = zeros
        field[:, :, PAD + size :] = zeros

    lower_half = lax.broadcasted_iota(jnp.int32, (1, 128), 1) < 64

    def both_edges(a):
        return jnp.where(lower_half, a[:, :128], a[:, width - 128 :])

    for copy in first_loads:
        copy.wait()
    for b in range(bands):
        high, low = split(strip[b])
        z = dot(rt[...], jnp.concatenate([high, low, high], 0))
        zsend_up[b] = z[0:8]
        zsend_down[b] = z[8:16]
        zown[b] = z[16:32]
        esend_up[b] = both_edges(z[0:8])
        esend_down[b] = both_edges(z[8:16])

    neighbours = (
        has_low_row.astype(jnp.int32)
        + has_high_row.astype(jnp.int32)
        + has_low_col.astype(jnp.int32)
        + has_high_col.astype(jnp.int32)
    )
    pl.semaphore_wait(barrier, neighbours)

    def exchange(axis, has_low, has_high, up, down, from_low, from_high, sem):
        here = lax.axis_index(axis)
        to_high = pltpu.make_async_remote_copy(
            up, from_low, sem.at[0], sem.at[1], device_id={axis: here + 1}, device_id_type=MESH
        )
        to_low = pltpu.make_async_remote_copy(
            down, from_high, sem.at[2], sem.at[3], device_id={axis: here - 1}, device_id_type=MESH
        )
        pl.when(has_high)(to_high.start)
        pl.when(has_low)(to_low.start)

        def arrive():
            pl.when(has_low)(to_high.wait_recv)
            pl.when(has_high)(to_low.wait_recv)

        def sent():
            pl.when(has_high)(to_high.wait_send)
            pl.when(has_low)(to_low.wait_send)

        return arrive, sent

    e_arrive, e_sent = exchange(
        "row", has_low_row, has_high_row, esend_up, esend_down, efrom_low, efrom_high, e_sem
    )
    z_arrive, z_sent = exchange(
        "row", has_low_row, has_high_row, zsend_up, zsend_down, zfrom_low, zfrom_high, z_sem
    )

    for b in range(bands):
        for copy in band_loads[b]:
            copy.wait()

        def reduce_tile(i, carry, b=b):
            for source, target in zip(fields[:LEVELS], ys):
                size = target.shape[2] - 2 * PAD
                tap = [source[b, i, pl.ds(PAD - 2 + t, size, stride=2)] for t in range(5)]
                target[b, i, PAD : PAD + size] = (
                    0.0625 * (tap[0] + tap[4]) + 0.25 * (tap[1] + tap[3]) + 0.375 * tap[2]
                )
            return carry

        lax.fori_loop(0, tiles, reduce_tile, 0, unroll=UNROLL)

    for copy in rest:
        copy.wait()
    for b in range(bands):
        for k, y in enumerate(ys):
            edge[b, starts[k] : starts[k] + sizes[k]] = jnp.where(
                lower_half, y[b, 0, PAD : PAD + sizes[k]], y[b, tiles - 1, PAD : PAD + sizes[k]]
            )
        edge[b, starts[LEVELS - 1] + sizes[LEVELS - 1] :] = jnp.zeros((sizes[LEVELS - 1], 128), jnp.float32)
    e_arrive()
    lane = lax.broadcasted_iota(jnp.int32, (8, height), 1)
    for b in range(bands):
        first = jnp.where(has_low_row, efrom_low[b], 0.0) + both_edges(zown[b, 0:8])
        last = jnp.where(has_high_row, efrom_high[b], 0.0) + both_edges(zown[b, 8:16])
        for k in range(LEVELS):
            begin, end = starts[k], starts[k] + sizes[k]
            edge[b, begin : begin + 2] = edge[b, begin : begin + 2] + first[2 * k : 2 * k + 2]
            edge[b, end - 1 : end] = edge[b, end - 1 : end] + last[k : k + 1]
        high, low = split(edge[b])
        v = lax.dot_general(
            ct[...],
            jnp.concatenate([high, low], 1),
            (((1,), (1,)), ((), ())),
            preferred_element_type=jnp.float32,
        )
        v = v[: 8 * LEVELS] + v[8 * LEVELS :]
        picked = v[8 * LEVELS - 8 :]
        for k in range(LEVELS - 2, -1, -1):
            picked = jnp.where(lane < starts[k + 1], v[8 * k : 8 * k + 8], picked)
        vsend[b] = picked
    v_arrive, v_sent = exchange(
        "col", has_low_col, has_high_col, vsend, vsend, vfrom_low, vfrom_high, v_sem
    )

    z_arrive()
    for b in range(bands):
        first = jnp.where(has_low_row, zfrom_low[b], 0.0) + zown[b, 0:8]
        last = jnp.where(has_high_row, zfrom_high[b], 0.0) + zown[b, 8:16]
        for k, y in enumerate(ys):
            for i in range(tiles):
                lanes = slice(128 * i, 128 * i + 128)
                y[b, i, PAD : PAD + 2] = y[b, i, PAD : PAD + 2] + first[2 * k : 2 * k + 2, lanes]
                end = slice(PAD + sizes[k] - 1, PAD + sizes[k])
                y[b, i, end] = y[b, i, end] + last[k : k + 1, lanes]

    rows = sum(sizes[1:]) * bands
    base = 0
    for k in range(1, LEVELS):
        for b in range(bands):
            for i in range(tiles):
                high, low = split(ys[k][b, i, PAD : PAD + sizes[k]])
                s234[base : base + sizes[k], 128 * i : 128 * i + 128] = high
                s234[rows + base : rows + base + sizes[k], 128 * i : 128 * i + 128] = low
            base += sizes[k]
    half = width // 2
    near = lax.broadcasted_iota(jnp.int32, (1, 128), 1)
    for b in range(bands):
        for i in range(tiles):
            high, low = split(y1[b, i, PAD : PAD + sizes[0]])
            h, lanes = divmod(128 * i, half)
            s1[2 * h * sizes[0] : (2 * h + 1) * sizes[0], lanes : lanes + 128] = high
            s1[(2 * h + 1) * sizes[0] : (2 * h + 2) * sizes[0], lanes : lanes + 128] = low
        one = dot(s1[...], c1[...])
        for h in range(2):
            o1[b, :, half // 2 * h : half // 2 * (h + 1)] = (
                one[2 * h * sizes[0] : (2 * h + 1) * sizes[0]]
                + one[(2 * h + 1) * sizes[0] : (2 * h + 2) * sizes[0]]
            )
        left = y1[b, tiles // 2 - 1, PAD : PAD + sizes[0]]
        right = y1[b, tiles // 2, PAD : PAD + sizes[0]]
        middle = half // 2
        o1[b, :, middle - 128 : middle] = o1[b, :, middle - 128 : middle] + jnp.where(
            near == 127, 0.0625 * pltpu.roll(right, 127, 1), 0.0
        )
        o1[b, :, middle : middle + 128] = o1[b, :, middle : middle + 128] + jnp.where(
            near == 0, 0.0625 * pltpu.roll(left, 2, 1) + 0.25 * pltpu.roll(left, 1, 1), 0.0
        )
    two = dot(s234[...], c12[...])
    two = two[:rows] + two[rows:]
    three = dot_split(two[bands * sizes[1] :], c3[...])
    four = dot_split(three[bands * sizes[2] :], c4[...])
    for b in range(bands):
        o2[b] = two[b * sizes[1] : (b + 1) * sizes[1]]
        o3[b] = three[b * sizes[2] : (b + 1) * sizes[2]]
        o4[b] = four[b * sizes[3] : (b + 1) * sizes[3], : width >> 4]

    v_arrive()
    at = lax.broadcasted_iota(jnp.int32, (128, 128), 1)
    row = lax.broadcasted_iota(jnp.int32, (8, height), 0)
    for b in range(bands):
        own = vsend[b]
        first = jnp.where(has_low_col, vfrom_low[b], 0.0) + pltpu.roll(own, 6, 0)
        last = jnp.where(has_high_col, pltpu.roll(vfrom_high[b], 2, 0), 0.0) + pltpu.roll(own, 3, 0)
        cells = jnp.where(row < 2, first, jnp.where(row == 7, last, 0.0))
        for part, levels in ((0, (0,)), (1, (1, 2, 3))):
            square = jnp.concatenate(
                [cells[:, 128 * part : 128 * part + 128], jnp.zeros((120, 128), jnp.float32)], 0
            ).T
            for k in levels:
                out = (o1, o2, o3, o4)[k]
                begin = starts[k] - 128 * part
                value = square[begin : begin + sizes[k]]
                tile = min(out.shape[2], 128)
                mark = at[: sizes[k]]
                low_cells = jnp.where(mark < 2, value, 0.0)[:, :tile]
                high_cells = jnp.where(mark == tile - 1, pltpu.roll(value, tile - 8, 1), 0.0)[:, :tile]
                out[b, :, 0:tile] = out[b, :, 0:tile] + low_cells
                out[b, :, out.shape[2] - tile :] = out[b, :, out.shape[2] - tile :] + high_cells
    e_sent()
    z_sent()
    v_sent()


def store_kernel(*refs):
    sources, targets, sem = refs[:LEVELS], refs[LEVELS : 2 * LEVELS], refs[2 * LEVELS]
    copies = [pltpu.make_async_copy(s, t, sem.at[k]) for k, (s, t) in enumerate(zip(sources, targets))]
    for copy in copies:
        copy.start()
    for copy in copies:
        copy.wait()


def solution(mesh):
    rows_n, cols_n = mesh.shape["row"], mesh.shape["col"]
    row_table, col_table = tables()

    def local(relief):
        bands, height, width = relief.shape
        f32, bf16 = jnp.float32, jnp.bfloat16
        c1 = reduce_matrix(width // 2, False).T
        c12 = chain(width, False)[1].T
        c3 = reduce_matrix(width // 4, False).T
        c4 = np.zeros((width // 8, 128))
        c4[:, : width // 16] = reduce_matrix(width // 8, False).T
        consts = [jnp.asarray(a, bf16) for a in (row_table, col_table, c1, c12, c3, c4)]
        shapes = [(bands, height >> k, width >> k) for k in range(1, LEVELS + 1)]

        vmem = lambda *shape, dtype=f32: pltpu.VMEM(shape, dtype)
        scratch = [vmem(bands, 2 * ROW_STRIP, width)]
        scratch += [vmem(bands, width // 128, (height >> k) + 2 * PAD, 128) for k in range(LEVELS + 1)]
        rest = sum(height >> k for k in range(2, LEVELS + 1))
        scratch += [
            vmem(2 * height, width // 2, dtype=bf16), vmem(2 * bands * rest, width, dtype=bf16),
            vmem(bands, height, 128),
        ]
        scratch += [vmem(*a.shape, dtype=bf16) for a in (row_table[0], col_table[0], c1, c12, c3, c4)]
        scratch += [vmem(bands, n, width) for n in (8, 8, 16, 8, 8)]
        scratch += [vmem(bands, 8, 128)] * 4
        scratch += [vmem(bands, 8, height)] * 3
        scratch += [
            pltpu.SemaphoreType.DMA(n) for n in ((2, bands), (bands, width // 128), (6,), (4,), (4,), (4,))
        ]
        held = pl.pallas_call(
            functools.partial(pyramid_kernel, rows_n, cols_n),
            out_shape=[jax.ShapeDtypeStruct(s, f32) for s in shapes],
            in_specs=[pl.BlockSpec(memory_space=pltpu.HBM)] * 7,
            out_specs=[pl.BlockSpec(memory_space=pltpu.VMEM)] * LEVELS,
            scratch_shapes=scratch,
            compiler_params=pltpu.CompilerParams(
                collective_id=0, has_side_effects=True, vmem_limit_bytes=40 << 20
            ),
            name="pyramid",
        )(*[pltpu.with_memory_space_constraint(a, pltpu.HBM) for a in (relief, *consts)])
        return pl.pallas_call(
            store_kernel,
            out_shape=[jax.ShapeDtypeStruct(s, f32) for s in shapes],
            in_specs=[pl.BlockSpec(memory_space=pltpu.VMEM)] * LEVELS,
            out_specs=[pl.BlockSpec(memory_space=pltpu.HBM)] * LEVELS,
            scratch_shapes=[pltpu.SemaphoreType.DMA((LEVELS,))],
            compiler_params=pltpu.CompilerParams(vmem_limit_bytes=16 << 20),
            name="store",
        )(*held)

    spec = P(None, "row", "col")
    return jax.shard_map(local, mesh=mesh, in_specs=(spec,), out_specs=(spec,) * LEVELS, check_vma=False)
```

time: 16.1 us -> 14.4 us (0.89)
  Pallas kernels: 15.3 us -> 13.6 us
    pallas_call x1, Pallas kernels: 14.4 us -> 12.7 us  [local(): pl.pallas_call(functools.partial(pyramid_kernel, rows_n, cols_n), out_sha...]
where the time goes in v2:
time: 14.4 us; the launch traced here: 14.3 us
  Pallas kernels  13.6 us (94%)
  between operations  0.64 us (4%)
    pallas_call x1, Pallas kernels, local(): pl.pallas_call(functools.partial(pyramid_kernel, rows_n, cols_n), out_sha...  12.7 us
    pallas_call x1, Pallas kernels, local(): pl.pallas_call(store_kernel, out_shape=[jax.ShapeDtypeStruct(s, f32) for...  0.99 us

profile of v2, /device:TPU:120, one launch (start us, length us, event | category | flops | bytes accessed | tf_op | source)
XLA Modules:
  0.0 14.3 jit_solution(15492238863519521604)
XLA Ops:
  0.6 12.7 %pyramid.1 = (f32[3,128,512]{2,1,0:T(8,128)S(1)}, f32[3,64,256]{2,1,0:T(8,128)S(1)}, f32[3,32,128]{2,1,0:T(8,128)S(1)}, f32[3,16,64]{2,1,0:T(8,128)S(1)}) custom-call(f32[3,256,1024]{2,1,0:T(8,128)} %x_hbm.1, bf16[3,32,192]{2,1,0:T(8,128)(2,1)} %constant.12.clone.rt_hbm, bf16[3,64,256]{2,1,0:T(8,128)(2,1)} %constant.13.clone.ct_hbm, ...), custom_call_target="tpu_custom_call" | custom-call | tf_op jit(solution)/shard_map/pyramid/pallas_call | solution.py:389
  13.3 1.0 %store.1 = (f32[3,128,512]{2,1,0:T(8,128)}, f32[3,64,256]{2,1,0:T(8,128)}, f32[3,32,128]{2,1,0:T(8,128)}, f32[3,16,64]{2,1,0:T(8,128)}) custom-call(f32[3,128,512]{2,1,0:T(8,128)S(1)} %get-tuple-element.8.refs_0_, f32[3,64,256]{2,1,0:T(8,128)S(1)} %get-tuple-element.9.refs_1_, f32[3,32,128]{2,1,0:T(8,128)S(1)} %get-tuple-element.10.refs_2_, ...), custom_call_target="tpu_custom_call" | custom-call | tf_op jit(solution)/shard_map/store/pallas_call | solution.py:400

commit v3 on v2

v3 whole, which is shorter than its diff:
```python
import functools

import jax
import jax.numpy as jnp
import numpy as np
from jax import lax
from jax.experimental import pallas as pl
from jax.experimental.pallas import tpu as pltpu
from jax.sharding import PartitionSpec as P

MESH = pl.DeviceIdType.MESH
BINOMIAL = np.array([1, 4, 6, 4, 1]) / 16
LEVELS = 4
PAD = 8
ROW_STRIP = 32
COL_STRIP = 64
UNROLL = 4


def reduce_matrix(n, reflect):
    d = np.zeros((n // 2, n))
    for i in range(n // 2):
        for t in range(5):
            c = 2 * i - 2 + t
            if c < 0 or c >= n:
                if not reflect:
                    continue
                c = -c if c < 0 else 2 * (n - 1) - c
            d[i, c] += BINOMIAL[t]
    return d


def chain(n, reflect):
    out, m = [], np.eye(n)
    for _ in range(LEVELS):
        m = reduce_matrix(m.shape[0], reflect) @ m
        out.append(m)
    return out


def edge_parts(n):
    whole, alone = chain(3 * n, True), chain(n, False)
    places = []
    for p in range(3):
        parts = []
        for k in range(LEVELS):
            m = n >> (k + 1)
            mine = whole[k][:, p * n : (p + 1) * n]
            own = mine[p * m : (p + 1) * m] - alone[k]
            assert not own[2:-1].any()
            up = mine[(p + 1) * m : (p + 1) * m + 2] if p < 2 else np.zeros((2, n))
            down = mine[p * m - 1 : p * m] if p > 0 else np.zeros((1, n))
            parts.append((up, down, own[:2], own[-1:]))
        places.append(parts)
    return places


def ends(rows, strip):
    return np.concatenate([rows[:, :strip], rows[:, -strip:]], 1)


def parts_of(table):
    high = np.asarray(jnp.asarray(table, jnp.bfloat16), np.float32)
    return high, table - high


def tables():
    places = edge_parts(256)
    row_table = np.zeros((3, 32, 2 * ROW_STRIP), np.float32)
    col_table = np.zeros((3, 8 * LEVELS, 2 * COL_STRIP), np.float32)
    for p, parts in enumerate(places):
        for k, (up, down, first, last) in enumerate(parts):
            row_table[p, 2 * k : 2 * k + 2] = ends(up, ROW_STRIP)
            row_table[p, 8 + 2 * k] = ends(down, ROW_STRIP)[0]
            row_table[p, 16 + 2 * k : 18 + 2 * k] = ends(first, ROW_STRIP)
            row_table[p, 24 + 2 * k] = ends(last, ROW_STRIP)[0]
            col_table[p, 8 * k : 8 * k + 6] = ends(np.concatenate([up, first, last, down]), COL_STRIP)
    high, low = parts_of(row_table)
    row_table = np.concatenate([high, high, low], 2)
    high, low = parts_of(col_table)
    none = np.zeros_like(low)
    col_table = np.concatenate(
        [np.concatenate([high, high], 2), np.concatenate([low, none], 2)], 1
    )
    return row_table, col_table


ABOVE = ((0, 1), (2, 3), (4, 5), (6, 7))
BELOW = (8, 10, 12, 14)


def whole_rows(n):
    whole = chain(3 * n, True)
    table = np.zeros((3, n, n + 128), np.float32)
    for p in range(3):
        for k in range(LEVELS):
            m, begin = n >> (k + 1), n - (n >> k)
            mine = whole[k][:, p * n : (p + 1) * n]
            table[p, :, begin : begin + m] = mine[p * m : (p + 1) * m].T
            if p < 2:
                for lane, cells in zip(ABOVE[k], mine[(p + 1) * m :]):
                    table[p, :, n + lane] = cells
            if p > 0:
                table[p, :, n + BELOW[k]] = mine[p * m - 1]
    return np.stack(parts_of(table), 1)


def split(a):
    high = a.astype(jnp.bfloat16)
    return high, (a - high.astype(jnp.float32)).astype(jnp.bfloat16)


dot = functools.partial(jnp.dot, preferred_element_type=jnp.float32)


def dot_split(a, weights):
    high, low = split(a)
    return dot(high, weights) + dot(low, weights)


def place(index, count):
    return jnp.where(index == 0, 0, jnp.where(index == count - 1, 2, 1))


def pyramid_kernel(
    rows_n, cols_n, x_hbm, rt_hbm, ct_hbm, wr_hbm, c1_hbm, c12_hbm, c3_hbm, c4_hbm,
    o1, o2, o3, o4, low_rows, high_rows, corners,
    strip, x, y1, y2, y3, y4, s1, s234, rt, ct, wr, c1, c12, c3, c4, zown,
    zsend_up, zsend_down, zfrom_low, zfrom_high,
    esend, efrom_low, efrom_high,
    vown, vsend_up, vsend_down, vfrom_low, vfrom_high,
    s_sem, x_sem, t_sem, e_sem, z_sem, v_sem, told,
):
    bands, height, width = x_hbm.shape
    tiles = width // 128
    r, c = lax.axis_index("row"), lax.axis_index("col")
    has_low_row, has_high_row = r > 0, r < rows_n - 1
    has_low_col, has_high_col = c > 0, c < cols_n - 1
    ys = (y1, y2, y3, y4)
    fields = (x,) + ys
    sizes = [height >> (k + 1) for k in range(LEVELS)]
    starts = [height - (height >> k) for k in range(LEVELS)]

    place_in_line = r % 8
    far_high = (place_in_line == 7) & has_high_row
    far_low = (place_in_line == 0) & has_low_row
    hears_high = (place_in_line == 6) & (r + 2 < rows_n)
    hears_low = (place_in_line == 1) & (r > 1)
    barrier = pltpu.get_barrier_semaphore()
    for axis, has, step in (
        ("row", has_low_row & jnp.logical_not(far_low), -1), ("row", has_high_row & jnp.logical_not(far_high), 1),
        ("row", far_low, -2), ("row", far_high, 2),
        ("col", has_low_col, -1), ("col", has_high_col, 1),
    ):

        @pl.when(has)
        def _(axis=axis, step=step):
            pl.semaphore_signal(
                barrier, inc=1, device_id={axis: lax.axis_index(axis) + step}, device_id_type=MESH
            )

    def load(source, target, sem):
        copy = pltpu.make_async_copy(source, target, sem)
        copy.start()
        return copy

    def load_tile(b, i):
        return load(x_hbm.at[b, :, 128 * i : 128 * i + 128], x.at[b, i, PAD : PAD + height], x_sem.at[b, i])

    col_loads = [load(ct_hbm.at[place(c, cols_n)], ct, t_sem.at[0])]
    for b in range(bands):
        col_loads += [load_tile(b, 0), load_tile(b, tiles - 1)]
    col_loads.append(load(wr_hbm.at[place(r, rows_n)], wr, t_sem.at[1]))
    row_loads = [load(rt_hbm.at[place(r, rows_n)], rt, t_sem.at[2])]
    for b in range(bands):
        for e, begin in enumerate((0, height - ROW_STRIP)):
            row_loads.append(
                load(
                    x_hbm.at[b, begin : begin + ROW_STRIP],
                    strip.at[b, e * ROW_STRIP : (e + 1) * ROW_STRIP],
                    s_sem.at[e, b],
                )
            )
    row_loads += [
        load(source, target, t_sem.at[3 + n])
        for n, (source, target) in enumerate(((c1_hbm, c1), (c12_hbm, c12), (c3_hbm, c3), (c4_hbm, c4)))
    ]
    band_loads = [[load_tile(b, i) for i in range(1, tiles - 1)] for b in range(bands)]

    for field in fields[:LEVELS]:
        size = field.shape[2] - 2 * PAD
        zeros = jnp.zeros((bands, tiles, PAD, 128), jnp.float32)
        field[:, :, 0:PAD] = zeros
        field[:, :, PAD + size :] = zeros

    lower_half = lax.broadcasted_iota(jnp.int32, (1, 128), 1) < 64
    for copy in col_loads:
        copy.wait()
    raw = []
    for b in range(bands):
        high, low = split(
            jnp.where(lower_half, x[b, 0, PAD : PAD + height], x[b, tiles - 1, PAD : PAD + height])
        )
        v = lax.dot_general(
            ct[...],
            jnp.concatenate([high, low], 1),
            (((1,), (1,)), ((), ())),
            preferred_element_type=jnp.float32,
        )
        raw.append(v[: 8 * LEVELS] + v[8 * LEVELS :])
    raw = jnp.concatenate(raw, 0)
    high, low = split(raw)
    v = dot(jnp.concatenate([high, low], 0), wr[0])
    v = v[: raw.shape[0]] + v[raw.shape[0] :] + dot(high, wr[1])
    lane = lax.broadcasted_iota(jnp.int32, (8, height + 128), 1)
    row = lax.broadcasted_iota(jnp.int32, (8, height + 128), 0)
    beyond = lane - height
    level_of = jnp.where(
        lane < height,
        sum((lane >= start).astype(jnp.int32) for start in starts[1:]),
        (beyond & 7) >> 1,
    )
    up, down = jnp.zeros(lane.shape, jnp.float32), jnp.zeros(lane.shape, jnp.float32)
    for b in range(bands):
        begin = 8 * LEVELS * b
        picked = v[begin : begin + 8]
        for k in range(1, LEVELS):
            picked = jnp.where(level_of == k, v[begin + 8 * k : begin + 8 * k + 8], picked)
        vown[b] = picked
        up = jnp.where((row >= 2 * b) & (row < 2 * b + 2), pltpu.roll(picked, 2 * b, 0), up)
        down = jnp.where(row == b, pltpu.roll(picked, b + 3, 0), down)
    vsend_up[...] = up
    vsend_down[...] = down

    expected = (
        (has_low_row & jnp.logical_not(far_low), has_high_row & jnp.logical_not(far_high))
        + (hears_low, hears_high, has_low_col, has_high_col)
    )
    pl.semaphore_wait(barrier, sum(has.astype(jnp.int32) for has in expected))
    for has, step in ((hears_high, 1), (hears_low, -1)):

        @pl.when(has)
        def _(step=step):
            pl.semaphore_signal(
                told, inc=1, device_id={"row": lax.axis_index("row") + step}, device_id_type=MESH
            )

    def exchange(axis, has_low, has_high, up, down, from_low, from_high, sem):
        here = lax.axis_index(axis)
        to_high = pltpu.make_async_remote_copy(
            up, from_low, sem.at[0], sem.at[1], device_id={axis: here + 1}, device_id_type=MESH
        )
        to_low = pltpu.make_async_remote_copy(
            down, from_high, sem.at[2], sem.at[3], device_id={axis: here - 1}, device_id_type=MESH
        )
        pl.when(has_high)(to_high.start)
        pl.when(has_low)(to_low.start)

        def arrive():
            pl.when(has_low)(to_high.wait_recv)
            pl.when(has_high)(to_low.wait_recv)

        def sent():
            pl.when(has_high)(to_high.wait_send)
            pl.when(has_low)(to_low.wait_send)

        return arrive, sent

    v_arrive, v_sent = exchange(
        "col", has_low_col, has_high_col, vsend_up, vsend_down, vfrom_low, vfrom_high, v_sem
    )

    half = width // 2
    near = lax.broadcasted_iota(jnp.int32, (1, 128), 1)

    def across_middle(out, left, right):
        before = out[0][:, half // 2 - 128 :] + jnp.where(near == 127, 0.0625 * pltpu.roll(right, 127, 1), 0.0)
        after = out[1][:, :128] + jnp.where(
            near == 0, 0.0625 * pltpu.roll(left, 2, 1) + 0.25 * pltpu.roll(left, 1, 1), 0.0
        )
        return jnp.concatenate([out[0][:, : half // 2 - 128], before], 1), jnp.concatenate(
            [after, out[1][:, 128:]], 1
        )

    for copy in row_loads:
        copy.wait()
    spilled = []
    for b in range(bands):
        high, low = split(strip[b])
        z = dot(rt[...], jnp.concatenate([high, low, high], 0))
        zown[b] = z[16:32]
        spilled.append(z[0:16])
    spilled = jnp.concatenate(spilled, 0)
    count = spilled.shape[0]
    high, low = split(spilled)
    one = dot(
        jnp.concatenate([high[:, :half], low[:, :half], high[:, half:], low[:, half:]], 0), c1[...]
    )
    one = across_middle(
        (one[:count] + one[count : 2 * count], one[2 * count : 3 * count] + one[3 * count :]),
        spilled[:, half - 128 : half],
        spilled[:, half : half + 128],
    )
    two = dot(jnp.concatenate([high, low], 0), c12[...])
    two = two[:count] + two[count:]
    three = dot_split(two, c3[...])
    four = dot_split(three, c4[...])
    for b in range(bands):
        for side, target in enumerate((zsend_up, zsend_down)):
            g = slice(16 * b + 8 * side, 16 * b + 8 * side + 8)
            pad = jnp.zeros((8, width // 4 - 128), jnp.float32)
            group = lax.broadcasted_iota(jnp.int32, (8, width // 4), 0)
            packed = jnp.where(group < 6, jnp.concatenate([three[g], pad], 1), jnp.concatenate([four[g], pad], 1))
            packed = jnp.where(group < 4, two[g], packed)
            packed = jnp.where(group == 1, pltpu.roll(one[1][g], 1, 0), packed)
            target[b] = jnp.where(group == 0, one[0][g], packed)
    pl.when(far_high | far_low)(lambda: pl.semaphore_wait(told, 1))
    z_arrive, z_sent = exchange(
        "row", has_low_row, has_high_row, zsend_up, zsend_down, zfrom_low, zfrom_high, z_sem
    )

    for b in range(bands):
        for copy in band_loads[b]:
            copy.wait()

        def reduce_tile(i, carry, b=b):
            for source, target in zip(fields[:LEVELS], ys):
                size = target.shape[2] - 2 * PAD
                tap = [source[b, i, pl.ds(PAD - 2 + t, size, stride=2)] for t in range(5)]
                target[b, i, PAD : PAD + size] = (
                    0.0625 * (tap[0] + tap[4]) + 0.25 * (tap[1] + tap[3]) + 0.375 * tap[2]
                )
            return carry

        lax.fori_loop(0, tiles, reduce_tile, 0, unroll=UNROLL)

    v_arrive()
    for b in range(bands):
        own = vown[b]
        low = jnp.where(has_low_col, vfrom_low[...], 0.0)
        high = jnp.where(has_high_col, vfrom_high[...], 0.0)
        first = pltpu.roll(own, 6, 0) + pltpu.roll(low, (8 - 2 * b) % 8, 0)
        last = pltpu.roll(own, 3, 0) + pltpu.roll(high, 7 - b, 0)
        both = jnp.where(row < 2, first, jnp.where(row == 7, last, 0.0))
        vown[b] = both
        esend[b] = both[:, height:]
    e_arrive, e_sent = exchange(
        "row", has_low_row, has_high_row, esend, esend, efrom_low, efrom_high, e_sem
    )

    for b in range(bands):
        for k, y in enumerate(ys):
            for i in range(tiles):
                lanes = slice(128 * i, 128 * i + 128)
                y[b, i, PAD : PAD + 2] = y[b, i, PAD : PAD + 2] + zown[b, 2 * k : 2 * k + 2, lanes]
                end = slice(PAD + sizes[k] - 1, PAD + sizes[k])
                y[b, i, end] = y[b, i, end] + zown[b, 8 + 2 * k : 9 + 2 * k, lanes]

    rows = sum(sizes[1:]) * bands
    base = 0
    for k in range(1, LEVELS):
        for b in range(bands):
            for i in range(tiles):
                high, low = split(ys[k][b, i, PAD : PAD + sizes[k]])
                s234[base : base + sizes[k], 128 * i : 128 * i + 128] = high
                s234[rows + base : rows + base + sizes[k], 128 * i : 128 * i + 128] = low
            base += sizes[k]
    for b in range(bands):
        for i in range(tiles):
            high, low = split(y1[b, i, PAD : PAD + sizes[0]])
            h, lanes = divmod(128 * i, half)
            s1[2 * h * sizes[0] : (2 * h + 1) * sizes[0], lanes : lanes + 128] = high
            s1[(2 * h + 1) * sizes[0] : (2 * h + 2) * sizes[0], lanes : lanes + 128] = low
        one = dot(s1[...], c1[...])
        size = sizes[0]
        one = across_middle(
            (one[:size] + one[size : 2 * size], one[2 * size : 3 * size] + one[3 * size :]),
            y1[b, tiles // 2 - 1, PAD : PAD + size],
            y1[b, tiles // 2, PAD : PAD + size],
        )
        o1[b, :, : half // 2] = one[0]
        o1[b, :, half // 2 :] = one[1]
    two = dot(s234[...], c12[...])
    two = two[:rows] + two[rows:]
    three = dot_split(two[bands * sizes[1] :], c3[...])
    four = dot_split(three[bands * sizes[2] :], c4[...])
    for b in range(bands):
        o2[b] = two[b * sizes[1] : (b + 1) * sizes[1]]
        o3[b] = three[b * sizes[2] : (b + 1) * sizes[2]]
        o4[b] = four[b * sizes[3] : (b + 1) * sizes[3], : width >> 4]

    at = lax.broadcasted_iota(jnp.int32, (128, 128), 1)
    for b in range(bands):
        for part, levels in ((0, (0,)), (1, (1, 2, 3))):
            square = jnp.concatenate(
                [vown[b, :, 128 * part : 128 * part + 128], jnp.zeros((120, 128), jnp.float32)], 0
            ).T
            for k in levels:
                out = (o1, o2, o3, o4)[k]
                begin = starts[k] - 128 * part
                value = square[begin : begin + sizes[k]]
                tile = min(out.shape[2], 128)
                mark = at[: sizes[k]]
                low_cells = jnp.where(mark < 2, value, 0.0)[:, :tile]
                high_cells = jnp.where(mark == tile - 1, pltpu.roll(value, tile - 8, 1), 0.0)[:, :tile]
                out[b, :, 0:tile] = out[b, :, 0:tile] + low_cells
                out[b, :, out.shape[2] - tile :] = out[b, :, out.shape[2] - tile :] + high_cells

    above = lax.broadcasted_iota(jnp.int32, (8, 128), 1) < 8
    z_arrive()
    for b in range(bands):
        low_rows[b] = jnp.where(has_low_row, zfrom_low[b], 0.0)
        high_rows[b] = jnp.where(has_high_row, zfrom_high[b], 0.0)
    e_arrive()
    for b in range(bands):
        corners[b] = jnp.where(
            above,
            jnp.where(has_low_row, efrom_low[b], 0.0),
            jnp.where(has_high_row, efrom_high[b], 0.0),
        )
    e_sent()
    z_sent()
    v_sent()


def store_kernel(a1, a2, a3, a4, low_rows, high_rows, corners, o1, o2, o3, o4, t1, t2, t3, t4, in_sem, edge_sem):
    bands = a1.shape[0]
    copies = []
    for k, (source, target) in enumerate(((a1, o1), (a2, o2), (a3, o3))):
        inner = slice(8, source.shape[1] - 8)
        copies.append(pltpu.make_async_copy(source.at[:, inner], target.at[:, inner], in_sem.at[k]))
        copies[-1].start()
    lane = lax.broadcasted_iota(jnp.int32, (16, 128), 1)
    for b in range(bands):
        cells = jnp.concatenate([corners[b], jnp.zeros((120, 128), jnp.float32)], 0).T[:16]
        first = jnp.where(lane < 2, cells, 0.0)
        last = jnp.where(lane == 127, pltpu.roll(cells, 120, 1), 0.0)
        last_half = jnp.where(lane == 63, pltpu.roll(cells, 56, 1), 0.0)
        for side, rows in enumerate((low_rows[b], high_rows[b])):
            for k, (source, target) in enumerate(zip((a1, a2, a3, a4), (t1, t2, t3, t4))):
                size, wide = source.shape[1:]
                count = 2 if side == 0 and k > 0 else 1
                at = slice(8 * side + 2 * k, 8 * side + 2 * k + count)
                if k == 0:
                    none = jnp.zeros((1, wide - 256), jnp.float32)
                    more = jnp.concatenate([rows[0:1], rows[1:2]], 1)
                    more = more + jnp.concatenate([first[at], none, last[at]], 1)
                else:
                    more = rows[2 * k : 2 * k + count, :wide]
                    if k == 1:
                        more = more + jnp.concatenate([first[at], last[at]], 1)
                    elif k == 2:
                        more = more + first[at] + last[at]
                    else:
                        more = more + (first[at] + last_half[at])[:, :wide]
                still = jnp.zeros((8 - count, wide), jnp.float32)
                if side == 0:
                    target[side, b] = source[b, 0:8] + jnp.concatenate([more, still], 0)
                else:
                    target[side, b] = source[b, size - 8 : size] + jnp.concatenate([still, more], 0)
    for k, (source, target) in enumerate(((t1, o1), (t2, o2), (t3, o3), (t4, o4))):
        size = target.shape[1]
        for side, begin in enumerate((0, size - 8)):
            copies.append(
                pltpu.make_async_copy(source.at[side], target.at[:, begin : begin + 8], edge_sem.at[side, k])
            )
            copies[-1].start()
    for copy in copies:
        copy.wait()


def solution(mesh):
    rows_n, cols_n = mesh.shape["row"], mesh.shape["col"]
    row_table, col_table = tables()
    all_rows = whole_rows(256)

    def local(relief):
        bands, height, width = relief.shape
        f32, bf16 = jnp.float32, jnp.bfloat16
        c1 = reduce_matrix(width // 2, False).T
        c12 = chain(width, False)[1].T
        c3 = reduce_matrix(width // 4, False).T
        c4 = np.zeros((width // 8, 128))
        c4[:, : width // 16] = reduce_matrix(width // 8, False).T
        consts = [jnp.asarray(a, bf16) for a in (row_table, col_table, all_rows, c1, c12, c3, c4)]
        shapes = [(bands, height >> k, width >> k) for k in range(1, LEVELS + 1)]

        vmem = lambda *shape, dtype=f32: pltpu.VMEM(shape, dtype)
        scratch = [vmem(bands, 2 * ROW_STRIP, width)]
        scratch += [vmem(bands, width // 128, (height >> k) + 2 * PAD, 128) for k in range(LEVELS + 1)]
        rest = sum(height >> k for k in range(2, LEVELS + 1))
        scratch += [
            vmem(2 * height, width // 2, dtype=bf16), vmem(2 * bands * rest, width, dtype=bf16),
        ]
        scratch += [vmem(*a.shape, dtype=bf16) for a in (row_table[0], col_table[0], all_rows[0], c1, c12, c3, c4)]
        scratch += [vmem(bands, 16, width)]
        scratch += [vmem(bands, 8, width // 4)] * 4
        scratch += [vmem(bands, 8, 128)] * 3
        scratch += [vmem(bands, 8, height + 128)] + [vmem(8, height + 128)] * 4
        scratch += [
            pltpu.SemaphoreType.DMA(n) for n in ((2, bands), (bands, width // 128), (7,), (4,), (4,), (4,))
        ]
        scratch += [pltpu.SemaphoreType.REGULAR]
        extra = [(bands, 8, width // 4)] * 2 + [(bands, 8, 128)]
        held = pl.pallas_call(
            functools.partial(pyramid_kernel, rows_n, cols_n),
            out_shape=[jax.ShapeDtypeStruct(s, f32) for s in shapes + extra],
            in_specs=[pl.BlockSpec(memory_space=pltpu.HBM)] * 8,
            out_specs=[pl.BlockSpec(memory_space=pltpu.VMEM)] * (LEVELS + 3),
            scratch_shapes=scratch,
            compiler_params=pltpu.CompilerParams(
                collective_id=0, has_side_effects=True, vmem_limit_bytes=40 << 20
            ),
            name="pyramid",
        )(*[pltpu.with_memory_space_constraint(a, pltpu.HBM) for a in (relief, *consts)])
        return pl.pallas_call(
            store_kernel,
            out_shape=[jax.ShapeDtypeStruct(s, f32) for s in shapes],
            in_specs=[pl.BlockSpec(memory_space=pltpu.VMEM)] * (LEVELS + 3),
            out_specs=[pl.BlockSpec(memory_space=pltpu.HBM)] * LEVELS,
            scratch_shapes=[vmem(2, bands, 8, across) for _, _, across in shapes]
            + [pltpu.SemaphoreType.DMA((LEVELS - 1,)), pltpu.SemaphoreType.DMA((2, LEVELS))],
            compiler_params=pltpu.CompilerParams(vmem_limit_bytes=16 << 20),
            name="store",
        )(*held)

    spec = P(None, "row", "col")
    return jax.shard_map(local, mesh=mesh, in_specs=(spec,), out_specs=(spec,) * LEVELS, check_vma=False)
```

time: 14.4 us -> 12.9 us (0.90)
  the two profiles are of different devices: /device:TPU:120 before, /device:TPU:121 now
where the time goes in v3:
time: 12.9 us; the launch traced here: 12.8 us
  Pallas kernels  12.2 us (95%)
  between operations  0.64 us (5%)
    pallas_call x1, Pallas kernels, local(): pl.pallas_call(functools.partial(pyramid_kernel, rows_n, cols_n), out_sha...  11.1 us
    pallas_call x1, Pallas kernels, local(): pl.pallas_call(store_kernel, out_shape=[jax.ShapeDtypeStruct(s, f32) for...  1.12 us

profile of v3, /device:TPU:121, one launch (start us, length us, event | category | flops | bytes accessed | tf_op | source)
XLA Modules:
  0.0 12.8 jit_solution(8023737404859643379)
XLA Ops:
  0.6 11.1 %pyramid.1 = (f32[3,128,512]{2,1,0:T(8,128)S(1)}, f32[3,64,256]{2,1,0:T(8,128)S(1)}, f32[3,32,128]{2,1,0:T(8,128)S(1)}, f32[3,16,64]{2,1,0:T(8,128)S(1)}, f32[3,...) custom-call(f32[3,256,1024]{2,1,0:T(8,128)} %x_hbm.1, ...), custom_call_target="tpu_custom_call" | custom-call | tf_op jit(solution)/shard_map/pyramid/pallas_call | solution.py:505
  11.7 1.1 %store.1 = (f32[3,128,512]{2,1,0:T(8,128)}, f32[3,64,256]{2,1,0:T(8,128)}, f32[3,32,128]{2,1,0:T(8,128)}, f32[3,16,64]{2,1,0:T(8,128)}) custom-call(f32[3,128,512]{2,1,0:T(8,128)S(1)} %get-tuple-element.11.a1, f32[3,64,256]{2,1,0:T(8,128)S(1)} %get-tuple-element.12.a2, f32[3,32,128]{2,1,0:T(8,128)S(1)} %get-tuple-element.13.a3, ...), custom_call_target="tpu_custom_call" | custom-call | tf_op jit(solution)/shard_map/store/pallas_call | solution.py:516

commit v4 on v3

--- a/solution.py
+++ b/solution.py
@@ -14,7 +14,8 @@
 PAD = 8
 ROW_STRIP = 32
 COL_STRIP = 64
-UNROLL = 4
+UNROLL = 2
+EARLY = 1
 
 
 def reduce_matrix(n, reflect):
@@ -164,13 +165,29 @@
         copy.start()
         return copy
 
+    def tile_copy(b, i):
+        return pltpu.make_async_copy(
+            x_hbm.at[b, :, 128 * i : 128 * i + 128], x.at[b, i, PAD : PAD + height], x_sem.at[b, i]
+        )
+
     def load_tile(b, i):
-        return load(x_hbm.at[b, :, 128 * i : 128 * i + 128], x.at[b, i, PAD : PAD + height], x_sem.at[b, i])
+        copy = tile_copy(b, i)
+        copy.start()
+        return copy
 
     col_loads = [load(ct_hbm.at[place(c, cols_n)], ct, t_sem.at[0])]
     for b in range(bands):
         col_loads += [load_tile(b, 0), load_tile(b, tiles - 1)]
-    col_loads.append(load(wr_hbm.at[place(r, rows_n)], wr, t_sem.at[1]))
+    wr_load = load(wr_hbm.at[place(r, rows_n)], wr, t_sem.at[1])
+    for field in fields[:LEVELS]:
+        size = field.shape[2] - 2 * PAD
+        zeros = jnp.zeros((bands, tiles, PAD, 128), jnp.float32)
+        field[:, :, 0:PAD] = zeros
+        field[:, :, PAD + size :] = zeros
+
+    lower_half = lax.broadcasted_iota(jnp.int32, (1, 128), 1) < 64
+    for copy in col_loads:
+        copy.wait()
     row_loads = [load(rt_hbm.at[place(r, rows_n)], rt, t_sem.at[2])]
     for b in range(bands):
         for e, begin in enumerate((0, height - ROW_STRIP)):
@@ -185,30 +202,29 @@
         load(source, target, t_sem.at[3 + n])
         for n, (source, target) in enumerate(((c1_hbm, c1), (c12_hbm, c12), (c3_hbm, c3), (c4_hbm, c4)))
     ]
-    band_loads = [[load_tile(b, i) for i in range(1, tiles - 1)] for b in range(bands)]
-
-    for field in fields[:LEVELS]:
-        size = field.shape[2] - 2 * PAD
-        zeros = jnp.zeros((bands, tiles, PAD, 128), jnp.float32)
-        field[:, :, 0:PAD] = zeros
-        field[:, :, PAD + size :] = zeros
-
-    lower_half = lax.broadcasted_iota(jnp.int32, (1, 128), 1) < 64
-    for copy in col_loads:
-        copy.wait()
-    raw = []
-    for b in range(bands):
-        high, low = split(
-            jnp.where(lower_half, x[b, 0, PAD : PAD + height], x[b, tiles - 1, PAD : PAD + height])
-        )
-        v = lax.dot_general(
-            ct[...],
-            jnp.concatenate([high, low], 1),
-            (((1,), (1,)), ((), ())),
-            preferred_element_type=jnp.float32,
-        )
-        raw.append(v[: 8 * LEVELS] + v[8 * LEVELS :])
+    for b in range(bands):
+        for i in range(1, tiles - 1):
+            tile_copy(b, i).start()
+    parts = []
+    for b in range(bands):
+        parts.append(
+            jnp.concatenate(
+                split(
+                    jnp.where(lower_half, x[b, 0, PAD : PAD + height], x[b, tiles - 1, PAD : PAD + height])
+                ),
+                1,
+            )
+        )
+    v = lax.dot_general(
+        ct[...],
+        jnp.concatenate(parts, 0),
+        (((1,), (1,)), ((), ())),
+        preferred_element_type=jnp.float32,
+    )
+    v = v[: 8 * LEVELS] + v[8 * LEVELS :]
+    raw = [v[:, b * height : (b + 1) * height] for b in range(bands)]
     raw = jnp.concatenate(raw, 0)
+    wr_load.wait()
     high, low = split(raw)
     v = dot(jnp.concatenate([high, low], 0), wr[0])
     v = v[: raw.shape[0]] + v[raw.shape[0] :] + dot(high, wr[1])
@@ -253,9 +269,6 @@
         to_low = pltpu.make_async_remote_copy(
             down, from_high, sem.at[2], sem.at[3], device_id={axis: here - 1}, device_id_type=MESH
         )
-        pl.when(has_high)(to_high.start)
-        pl.when(has_low)(to_low.start)
-
         def arrive():
             pl.when(has_low)(to_high.wait_recv)
             pl.when(has_high)(to_low.wait_recv)
@@ -264,11 +277,13 @@
             pl.when(has_high)(to_high.wait_send)
             pl.when(has_low)(to_low.wait_send)
 
-        return arrive, sent
-
-    v_arrive, v_sent = exchange(
+        return to_high, to_low, arrive, sent
+
+    v_high, v_low, v_arrive, v_sent = exchange(
         "col", has_low_col, has_high_col, vsend_up, vsend_down, vfrom_low, vfrom_high, v_sem
     )
+    pl.when(has_low_col)(v_low.start)
+    pl.when(has_high_col)(v_high.start)
 
     half = width // 2
     near = lax.broadcasted_iota(jnp.int32, (1, 128), 1)
@@ -288,7 +303,8 @@
     for b in range(bands):
         high, low = split(strip[b])
         z = dot(rt[...], jnp.concatenate([high, low, high], 0))
-        zown[b] = z[16:32]
+        for i in range(tiles):
+            zown[b, i] = z[16:32, 128 * i : 128 * i + 128]
         spilled.append(z[0:16])
     spilled = jnp.concatenate(spilled, 0)
     count = spilled.shape[0]
@@ -315,62 +331,70 @@
             packed = jnp.where(group == 1, pltpu.roll(one[1][g], 1, 0), packed)
             target[b] = jnp.where(group == 0, one[0][g], packed)
     pl.when(far_high | far_low)(lambda: pl.semaphore_wait(told, 1))
-    z_arrive, z_sent = exchange(
+    z_high, z_low, z_arrive, z_sent = exchange(
         "row", has_low_row, has_high_row, zsend_up, zsend_down, zfrom_low, zfrom_high, z_sem
     )
-
-    for b in range(bands):
-        for copy in band_loads[b]:
-            copy.wait()
-
-        def reduce_tile(i, carry, b=b):
+    pl.when(has_high_row)(z_high.start)
+    pl.when(has_low_row)(z_low.start)
+    e_high, e_low, e_arrive, e_sent = exchange(
+        "row", has_low_row, has_high_row, esend, esend, efrom_low, efrom_high, e_sem
+    )
+
+    def forward():
+        v_arrive()
+        low = jnp.where(has_low_col, vfrom_low[...], 0.0)
+        high = jnp.where(has_high_col, vfrom_high[...], 0.0)
+        for b in range(bands):
+            own = vown[b]
+            first = pltpu.roll(own, 6, 0) + pltpu.roll(low, (8 - 2 * b) % 8, 0)
+            last = pltpu.roll(own, 3, 0) + pltpu.roll(high, 7 - b, 0)
+            both = jnp.where(row < 2, first, jnp.where(row == 7, last, 0.0))
+            vown[b] = both
+            esend[b] = both[:, height:]
+        pl.when(has_high_row)(e_high.start)
+        pl.when(has_low_row)(e_low.start)
+
+    def reduce_band(b, carry):
+        pl.when(late & (b == EARLY))(forward)
+        for i in range(1, tiles - 1):
+            tile_copy(b, i).wait()
+
+        def reduce_tile(i, carry):
             for source, target in zip(fields[:LEVELS], ys):
                 size = target.shape[2] - 2 * PAD
                 tap = [source[b, i, pl.ds(PAD - 2 + t, size, stride=2)] for t in range(5)]
                 target[b, i, PAD : PAD + size] = (
                     0.0625 * (tap[0] + tap[4]) + 0.25 * (tap[1] + tap[3]) + 0.375 * tap[2]
                 )
+            for k, y in enumerate(ys):
+                y[b, i, PAD : PAD + 2] = y[b, i, PAD : PAD + 2] + zown[b, i, 2 * k : 2 * k + 2]
+                end = slice(PAD + sizes[k] - 1, PAD + sizes[k])
+                y[b, i, end] = y[b, i, end] + zown[b, i, 8 + 2 * k : 9 + 2 * k]
             return carry
 
         lax.fori_loop(0, tiles, reduce_tile, 0, unroll=UNROLL)
-
-    v_arrive()
-    for b in range(bands):
-        own = vown[b]
-        low = jnp.where(has_low_col, vfrom_low[...], 0.0)
-        high = jnp.where(has_high_col, vfrom_high[...], 0.0)
-        first = pltpu.roll(own, 6, 0) + pltpu.roll(low, (8 - 2 * b) % 8, 0)
-        last = pltpu.roll(own, 3, 0) + pltpu.roll(high, 7 - b, 0)
-        both = jnp.where(row < 2, first, jnp.where(row == 7, last, 0.0))
-        vown[b] = both
-        esend[b] = both[:, height:]
-    e_arrive, e_sent = exchange(
-        "row", has_low_row, has_high_row, esend, esend, efrom_low, efrom_high, e_sem
-    )
-
-    for b in range(bands):
-        for k, y in enumerate(ys):
-            for i in range(tiles):
-                lanes = slice(128 * i, 128 * i + 128)
-                y[b, i, PAD : PAD + 2] = y[b, i, PAD : PAD + 2] + zown[b, 2 * k : 2 * k + 2, lanes]
-                end = slice(PAD + sizes[k] - 1, PAD + sizes[k])
-                y[b, i, end] = y[b, i, end] + zown[b, 8 + 2 * k : 9 + 2 * k, lanes]
-
-    rows = sum(sizes[1:]) * bands
-    base = 0
-    for k in range(1, LEVELS):
-        for b in range(bands):
+        return carry
+
+    late = c >= cols_n // 2
+    lax.fori_loop(0, bands, reduce_band, 0)
+    pl.when(jnp.logical_not(late))(forward)
+
+    rest = sum(sizes[1:])
+    at = lax.broadcasted_iota(jnp.int32, (128, 128), 1)
+
+    def reduce_columns(b, carry):
+        base = 0
+        for k in range(LEVELS):
             for i in range(tiles):
                 high, low = split(ys[k][b, i, PAD : PAD + sizes[k]])
-                s234[base : base + sizes[k], 128 * i : 128 * i + 128] = high
-                s234[rows + base : rows + base + sizes[k], 128 * i : 128 * i + 128] = low
-            base += sizes[k]
-    for b in range(bands):
-        for i in range(tiles):
-            high, low = split(y1[b, i, PAD : PAD + sizes[0]])
-            h, lanes = divmod(128 * i, half)
-            s1[2 * h * sizes[0] : (2 * h + 1) * sizes[0], lanes : lanes + 128] = high
-            s1[(2 * h + 1) * sizes[0] : (2 * h + 2) * sizes[0], lanes : lanes + 128] = low
+                if k == 0:
+                    h, lanes = divmod(128 * i, half)
+                    s1[2 * h * sizes[0] : (2 * h + 1) * sizes[0], lanes : lanes + 128] = high
+                    s1[(2 * h + 1) * sizes[0] : (2 * h + 2) * sizes[0], lanes : lanes + 128] = low
+                else:
+                    s234[base : base + sizes[k], 128 * i : 128 * i + 128] = high
+                    s234[rest + base : rest + base + sizes[k], 128 * i : 128 * i + 128] = low
+            base += sizes[k] if k else 0
         one = dot(s1[...], c1[...])
         size = sizes[0]
         one = across_middle(
@@ -380,17 +404,13 @@
         )
         o1[b, :, : half // 2] = one[0]
         o1[b, :, half // 2 :] = one[1]
-    two = dot(s234[...], c12[...])
-    two = two[:rows] + two[rows:]
-    three = dot_split(two[bands * sizes[1] :], c3[...])
-    four = dot_split(three[bands * sizes[2] :], c4[...])
-    for b in range(bands):
-        o2[b] = two[b * sizes[1] : (b + 1) * sizes[1]]
-        o3[b] = three[b * sizes[2] : (b + 1) * sizes[2]]
-        o4[b] = four[b * sizes[3] : (b + 1) * sizes[3], : width >> 4]
-
-    at = lax.broadcasted_iota(jnp.int32, (128, 128), 1)
-    for b in range(bands):
+        two = dot(s234[...], c12[...])
+        two = two[:rest] + two[rest:]
+        three = dot_split(two[sizes[1] :], c3[...])
+        four = dot_split(three[sizes[2] :], c4[...])
+        o2[b] = two[: sizes[1]]
+        o3[b] = three[: sizes[2]]
+        o4[b] = four[:, : width >> 4]
         for part, levels in ((0, (0,)), (1, (1, 2, 3))):
             square = jnp.concatenate(
                 [vown[b, :, 128 * part : 128 * part + 128], jnp.zeros((120, 128), jnp.float32)], 0
@@ -405,6 +425,9 @@
                 high_cells = jnp.where(mark == tile - 1, pltpu.roll(value, tile - 8, 1), 0.0)[:, :tile]
                 out[b, :, 0:tile] = out[b, :, 0:tile] + low_cells
                 out[b, :, out.shape[2] - tile :] = out[b, :, out.shape[2] - tile :] + high_cells
+        return carry
+
+    lax.fori_loop(0, bands, reduce_columns, 0)
 
     above = lax.broadcasted_iota(jnp.int32, (8, 128), 1) < 8
     z_arrive()
@@ -490,10 +513,10 @@
         scratch += [vmem(bands, width // 128, (height >> k) + 2 * PAD, 128) for k in range(LEVELS + 1)]
         rest = sum(height >> k for k in range(2, LEVELS + 1))
         scratch += [
-            vmem(2 * height, width // 2, dtype=bf16), vmem(2 * bands * rest, width, dtype=bf16),
+            vmem(2 * height, width // 2, dtype=bf16), vmem(2 * rest, width, dtype=bf16),
         ]
         scratch += [vmem(*a.shape, dtype=bf16) for a in (row_table[0], col_table[0], all_rows[0], c1, c12, c3, c4)]
-        scratch += [vmem(bands, 16, width)]
+        scratch += [vmem(bands, width // 128, 16, 128)]
         scratch += [vmem(bands, 8, width // 4)] * 4
         scratch += [vmem(bands, 8, 128)] * 3
         scratch += [vmem(bands, 8, height + 128)] + [vmem(8, height + 128)] * 4

time: 12.9 us -> 12.4 us (0.961)
  the two profiles are of different devices: /device:TPU:121 before, /device:TPU:71 now
where the time goes in v4:
time: 12.4 us; the launch traced here: 12.3 us
  Pallas kernels  11.6 us (94%)
  between operations  0.64 us (5%)
    pallas_call x1, Pallas kernels, local(): pl.pallas_call(functools.partial(pyramid_kernel, rows_n, cols_n), out_sha...  10.5 us
    pallas_call x1, Pallas kernels, local(): pl.pallas_call(store_kernel, out_shape=[jax.ShapeDtypeStruct(s, f32) for...  1.12 us

profile of v4, /device:TPU:71, one launch (start us, length us, event | category | flops | bytes accessed | tf_op | source)
XLA Modules:
  0.0 12.3 jit_solution(9353684154492461247)
XLA Ops:
  0.6 10.5 %pyramid.1 = (f32[3,128,512]{2,1,0:T(8,128)S(1)}, f32[3,64,256]{2,1,0:T(8,128)S(1)}, f32[3,32,128]{2,1,0:T(8,128)S(1)}, f32[3,16,64]{2,1,0:T(8,128)S(1)}, f32[3,...) custom-call(f32[3,256,1024]{2,1,0:T(8,128)} %x_hbm.1, ...), custom_call_target="tpu_custom_call" | custom-call | tf_op jit(solution)/shard_map/pyramid/pallas_call | solution.py:528
  11.2 1.1 %store.1 = (f32[3,128,512]{2,1,0:T(8,128)}, f32[3,64,256]{2,1,0:T(8,128)}, f32[3,32,128]{2,1,0:T(8,128)}, f32[3,16,64]{2,1,0:T(8,128)}) custom-call(f32[3,128,512]{2,1,0:T(8,128)S(1)} %get-tuple-element.11.a1, f32[3,64,256]{2,1,0:T(8,128)S(1)} %get-tuple-element.12.a2, f32[3,32,128]{2,1,0:T(8,128)S(1)} %get-tuple-element.13.a3, ...), custom_call_target="tpu_custom_call" | custom-call | tf_op jit(solution)/shard_map/store/pallas_call | solution.py:539

commit v5 on v4

--- a/solution.py
+++ b/solution.py
@@ -124,9 +124,9 @@
 
 
 def pyramid_kernel(
-    rows_n, cols_n, x_hbm, rt_hbm, ct_hbm, wr_hbm, c1_hbm, c12_hbm, c3_hbm, c4_hbm,
+    rows_n, cols_n, x_hbm, rt_hbm, ct_hbm, wr_hbm, cc_hbm,
     o1, o2, o3, o4, low_rows, high_rows, corners,
-    strip, x, y1, y2, y3, y4, s1, s234, rt, ct, wr, c1, c12, c3, c4, zown,
+    strip, x, y1, y2, y3, y4, s1, s234, rt, ct, wr, cc, zown,
     zsend_up, zsend_down, zfrom_low, zfrom_high,
     esend, efrom_low, efrom_high,
     vown, vsend_up, vsend_down, vfrom_low, vfrom_high,
@@ -165,20 +165,16 @@
         copy.start()
         return copy
 
-    def tile_copy(b, i):
-        return pltpu.make_async_copy(
-            x_hbm.at[b, :, 128 * i : 128 * i + 128], x.at[b, i, PAD : PAD + height], x_sem.at[b, i]
-        )
-
-    def load_tile(b, i):
-        copy = tile_copy(b, i)
-        copy.start()
-        return copy
-
-    col_loads = [load(ct_hbm.at[place(c, cols_n)], ct, t_sem.at[0])]
-    for b in range(bands):
-        col_loads += [load_tile(b, 0), load_tile(b, tiles - 1)]
+    def load_tile(i, sem):
+        return load(x_hbm.at[:, :, 128 * i : 128 * i + 128], x.at[:, i, PAD : PAD + height], sem)
+
+    col_loads = [
+        load(ct_hbm.at[place(c, cols_n)], ct, t_sem.at[0]),
+        load_tile(0, x_sem.at[0]),
+        load_tile(tiles - 1, x_sem.at[1]),
+    ]
     wr_load = load(wr_hbm.at[place(r, rows_n)], wr, t_sem.at[1])
+
     for field in fields[:LEVELS]:
         size = field.shape[2] - 2 * PAD
         zeros = jnp.zeros((bands, tiles, PAD, 128), jnp.float32)
@@ -189,22 +185,20 @@
     for copy in col_loads:
         copy.wait()
     row_loads = [load(rt_hbm.at[place(r, rows_n)], rt, t_sem.at[2])]
-    for b in range(bands):
-        for e, begin in enumerate((0, height - ROW_STRIP)):
-            row_loads.append(
-                load(
-                    x_hbm.at[b, begin : begin + ROW_STRIP],
-                    strip.at[b, e * ROW_STRIP : (e + 1) * ROW_STRIP],
-                    s_sem.at[e, b],
-                )
+    for e, begin in enumerate((0, height - ROW_STRIP)):
+        row_loads.append(
+            load(
+                x_hbm.at[:, begin : begin + ROW_STRIP],
+                strip.at[:, e * ROW_STRIP : (e + 1) * ROW_STRIP],
+                s_sem.at[e],
             )
-    row_loads += [
-        load(source, target, t_sem.at[3 + n])
-        for n, (source, target) in enumerate(((c1_hbm, c1), (c12_hbm, c12), (c3_hbm, c3), (c4_hbm, c4)))
-    ]
-    for b in range(bands):
-        for i in range(1, tiles - 1):
-            tile_copy(b, i).start()
+        )
+    row_loads.append(load(cc_hbm, cc, t_sem.at[3]))
+    for i in range(1, tiles - 1):
+        load_tile(i, x_sem.at[2])
+    c12, c1 = cc.at[0:width], cc.at[width : width + width // 2]
+    tail = width + width // 2
+    c3, c4 = cc.at[tail : tail + width // 4, 0:128], cc.at[tail : tail + width // 8, 128:256]
     parts = []
     for b in range(bands):
         parts.append(
@@ -356,9 +350,6 @@
 
     def reduce_band(b, carry):
         pl.when(late & (b == EARLY))(forward)
-        for i in range(1, tiles - 1):
-            tile_copy(b, i).wait()
-
         def reduce_tile(i, carry):
             for source, target in zip(fields[:LEVELS], ys):
                 size = target.shape[2] - 2 * PAD
@@ -376,6 +367,8 @@
         return carry
 
     late = c >= cols_n // 2
+    inner = x.at[:, 1 : tiles - 1, PAD : PAD + height]
+    pltpu.make_async_copy(inner, inner, x_sem.at[2]).wait()
     lax.fori_loop(0, bands, reduce_band, 0)
     pl.when(jnp.logical_not(late))(forward)
 
@@ -484,10 +477,8 @@
     for k, (source, target) in enumerate(((t1, o1), (t2, o2), (t3, o3), (t4, o4))):
         size = target.shape[1]
         for side, begin in enumerate((0, size - 8)):
-            copies.append(
-                pltpu.make_async_copy(source.at[side], target.at[:, begin : begin + 8], edge_sem.at[side, k])
-            )
-            copies[-1].start()
+            pltpu.make_async_copy(source.at[side], target.at[:, begin : begin + 8], edge_sem.at[k]).start()
+        copies.append(pltpu.make_async_copy(source, source, edge_sem.at[k]))
     for copy in copies:
         copy.wait()
 
@@ -503,9 +494,10 @@
         c1 = reduce_matrix(width // 2, False).T
         c12 = chain(width, False)[1].T
         c3 = reduce_matrix(width // 4, False).T
-        c4 = np.zeros((width // 8, 128))
-        c4[:, : width // 16] = reduce_matrix(width // 8, False).T
-        consts = [jnp.asarray(a, bf16) for a in (row_table, col_table, all_rows, c1, c12, c3, c4)]
+        c4 = np.zeros((width // 4, 128))
+        c4[: width // 8, : width // 16] = reduce_matrix(width // 8, False).T
+        cc = np.concatenate([c12, c1, np.concatenate([c3, c4], 1)], 0)
+        consts = [jnp.asarray(a, bf16) for a in (row_table, col_table, all_rows, cc)]
         shapes = [(bands, height >> k, width >> k) for k in range(1, LEVELS + 1)]
 
         vmem = lambda *shape, dtype=f32: pltpu.VMEM(shape, dtype)
@@ -515,20 +507,20 @@
         scratch += [
             vmem(2 * height, width // 2, dtype=bf16), vmem(2 * rest, width, dtype=bf16),
         ]
-        scratch += [vmem(*a.shape, dtype=bf16) for a in (row_table[0], col_table[0], all_rows[0], c1, c12, c3, c4)]
+        scratch += [vmem(*a.shape, dtype=bf16) for a in (row_table[0], col_table[0], all_rows[0], cc)]
         scratch += [vmem(bands, width // 128, 16, 128)]
         scratch += [vmem(bands, 8, width // 4)] * 4
         scratch += [vmem(bands, 8, 128)] * 3
         scratch += [vmem(bands, 8, height + 128)] + [vmem(8, height + 128)] * 4
         scratch += [
-            pltpu.SemaphoreType.DMA(n) for n in ((2, bands), (bands, width // 128), (7,), (4,), (4,), (4,))
+            pltpu.SemaphoreType.DMA(n) for n in ((2,), (3,), (4,), (4,), (4,), (4,))
         ]
         scratch += [pltpu.SemaphoreType.REGULAR]
         extra = [(bands, 8, width // 4)] * 2 + [(bands, 8, 128)]
         held = pl.pallas_call(
             functools.partial(pyramid_kernel, rows_n, cols_n),
             out_shape=[jax.ShapeDtypeStruct(s, f32) for s in shapes + extra],
-            in_specs=[pl.BlockSpec(memory_space=pltpu.HBM)] * 8,
+            in_specs=[pl.BlockSpec(memory_space=pltpu.HBM)] * 5,
             out_specs=[pl.BlockSpec(memory_space=pltpu.VMEM)] * (LEVELS + 3),
             scratch_shapes=scratch,
             compiler_params=pltpu.CompilerParams(
@@ -542,7 +534,7 @@
             in_specs=[pl.BlockSpec(memory_space=pltpu.VMEM)] * (LEVELS + 3),
             out_specs=[pl.BlockSpec(memory_space=pltpu.HBM)] * LEVELS,
             scratch_shapes=[vmem(2, bands, 8, across) for _, _, across in shapes]
-            + [pltpu.SemaphoreType.DMA((LEVELS - 1,)), pltpu.SemaphoreType.DMA((2, LEVELS))],
+            + [pltpu.SemaphoreType.DMA((LEVELS - 1,)), pltpu.SemaphoreType.DMA((LEVELS,))],
             compiler_params=pltpu.CompilerParams(vmem_limit_bytes=16 << 20),
             name="store",
         )(*held)

time: 12.4 us -> 12.1 us (0.976)
  Pallas kernels: 11.6 us -> 11.4 us
    pallas_call x1, Pallas kernels: 10.5 us -> 10.3 us  [local(): pl.pallas_call(functools.partial(pyramid_kernel, rows_n, cols_n), out_sha...]
where the time goes in v5:
time: 12.1 us; the launch traced here: 12 us
  Pallas kernels  11.4 us (94%)
  between operations  0.64 us (5%)
    pallas_call x1, Pallas kernels, local(): pl.pallas_call(functools.partial(pyramid_kernel, rows_n, cols_n), out_sha...  10.3 us
    pallas_call x1, Pallas kernels, local(): pl.pallas_call(store_kernel, out_shape=[jax.ShapeDtypeStruct(s, f32) for...  1.08 us

profile of v5, /device:TPU:71, one launch (start us, length us, event | category | flops | bytes accessed | tf_op | source)
XLA Modules:
  0.0 12.0 jit_solution(2052311684294611262)
XLA Ops:
  0.6 10.3 %pyramid.1 = (f32[3,128,512]{2,1,0:T(8,128)S(1)}, f32[3,64,256]{2,1,0:T(8,128)S(1)}, f32[3,32,128]{2,1,0:T(8,128)S(1)}, f32[3,16,64]{2,1,0:T(8,128)S(1)}, f32[3,...) custom-call(f32[3,256,1024]{2,1,0:T(8,128)} %x_hbm.1, ...), custom_call_target="tpu_custom_call" | custom-call | tf_op jit(solution)/shard_map/pyramid/pallas_call | solution.py:520
  10.9 1.1 %store.1 = (f32[3,128,512]{2,1,0:T(8,128)}, f32[3,64,256]{2,1,0:T(8,128)}, f32[3,32,128]{2,1,0:T(8,128)}, f32[3,16,64]{2,1,0:T(8,128)}) custom-call(f32[3,128,512]{2,1,0:T(8,128)S(1)} %get-tuple-element.11.a1, f32[3,64,256]{2,1,0:T(8,128)S(1)} %get-tuple-element.12.a2, f32[3,32,128]{2,1,0:T(8,128)S(1)} %get-tuple-element.13.a3, ...), custom_call_target="tpu_custom_call" | custom-call | tf_op jit(solution)/shard_map/store/pallas_call | solution.py:531

commit v6 on v5

--- a/solution.py
+++ b/solution.py
@@ -14,7 +14,9 @@
 PAD = 8
 ROW_STRIP = 32
 COL_STRIP = 64
-UNROLL = 2
+UNROLL = 4
+DIRECT = 4
+FORWARD = 1
 EARLY = 1
 
 
@@ -129,8 +131,8 @@
     strip, x, y1, y2, y3, y4, s1, s234, rt, ct, wr, cc, zown,
     zsend_up, zsend_down, zfrom_low, zfrom_high,
     esend, efrom_low, efrom_high,
-    vown, vsend_up, vsend_down, vfrom_low, vfrom_high,
-    s_sem, x_sem, t_sem, e_sem, z_sem, v_sem, told,
+    vown, vsend_up, vsend_down, vfrom_low, vfrom_high, dfrom_low, dfrom_high,
+    s_sem, x_sem, t_sem, e_sem, z_sem, v_sem, d_sem, told,
 ):
     bands, height, width = x_hbm.shape
     tiles = width // 128
@@ -147,6 +149,9 @@
     far_low = (place_in_line == 0) & has_low_row
     hears_high = (place_in_line == 6) & (r + 2 < rows_n)
     hears_low = (place_in_line == 1) & (r > 1)
+    middle = cols_n // 2
+    direct = (c >= middle - DIRECT) & (c < middle) & has_high_col
+    sends_diagonal = (c > middle - DIRECT) & (c <= middle) & has_low_col
     barrier = pltpu.get_barrier_semaphore()
     for axis, has, step in (
         ("row", has_low_row & jnp.logical_not(far_low), -1), ("row", has_high_row & jnp.logical_not(far_high), 1),
@@ -159,6 +164,12 @@
             pl.semaphore_signal(
                 barrier, inc=1, device_id={axis: lax.axis_index(axis) + step}, device_id_type=MESH
             )
+
+    for has, step in ((has_low_row, -1), (has_high_row, 1)):
+
+        @pl.when(has & direct)
+        def _(step=step):
+            pl.semaphore_signal(barrier, inc=1, device_id={"row": r + step, "col": c + 1}, device_id_type=MESH)
 
     def load(source, target, sem):
         copy = pltpu.make_async_copy(source, target, sem)
@@ -244,7 +255,7 @@
 
     expected = (
         (has_low_row & jnp.logical_not(far_low), has_high_row & jnp.logical_not(far_high))
-        + (hears_low, hears_high, has_low_col, has_high_col)
+        + (hears_low, hears_high, has_low_col, has_high_col, sends_diagonal & has_low_row, sends_diagonal & has_high_row)
     )
     pl.semaphore_wait(barrier, sum(has.astype(jnp.int32) for has in expected))
     for has, step in ((hears_high, 1), (hears_low, -1)):
@@ -278,6 +289,15 @@
     )
     pl.when(has_low_col)(v_low.start)
     pl.when(has_high_col)(v_high.start)
+    diagonals = []
+    for n, (has, step, target) in enumerate(((has_high_row, 1, dfrom_low), (has_low_row, -1, dfrom_high))):
+        diagonals.append(
+            pltpu.make_async_remote_copy(
+                vsend_down.at[:, height:], target, d_sem.at[2 * n], d_sem.at[2 * n + 1],
+                device_id={"row": r + step, "col": c - 1}, device_id_type=MESH,
+            )
+        )
+        pl.when(sends_diagonal & has)(diagonals[-1].start)
 
     half = width // 2
     near = lax.broadcasted_iota(jnp.int32, (1, 128), 1)
@@ -330,26 +350,34 @@
     )
     pl.when(has_high_row)(z_high.start)
     pl.when(has_low_row)(z_low.start)
+
     e_high, e_low, e_arrive, e_sent = exchange(
         "row", has_low_row, has_high_row, esend, esend, efrom_low, efrom_high, e_sem
     )
 
-    def forward():
-        v_arrive()
+    def forward(with_high=True):
+        pl.when(has_low_col)(v_high.wait_recv)
         low = jnp.where(has_low_col, vfrom_low[...], 0.0)
-        high = jnp.where(has_high_col, vfrom_high[...], 0.0)
+        if with_high:
+            pl.when(has_high_col)(v_low.wait_recv)
+            high = jnp.where(has_high_col, vfrom_high[...], 0.0)
         for b in range(bands):
             own = vown[b]
             first = pltpu.roll(own, 6, 0) + pltpu.roll(low, (8 - 2 * b) % 8, 0)
-            last = pltpu.roll(own, 3, 0) + pltpu.roll(high, 7 - b, 0)
+            last = pltpu.roll(own, 3, 0)
+            if with_high:
+                last = last + pltpu.roll(high, 7 - b, 0)
             both = jnp.where(row < 2, first, jnp.where(row == 7, last, 0.0))
             vown[b] = both
             esend[b] = both[:, height:]
         pl.when(has_high_row)(e_high.start)
         pl.when(has_low_row)(e_low.start)
 
-    def reduce_band(b, carry):
-        pl.when(late & (b == EARLY))(forward)
+    def reduce_band(b):
+        if b == FORWARD:
+            pl.when(direct)(lambda: forward(False))
+        if b == EARLY:
+            pl.when(late)(forward)
         def reduce_tile(i, carry):
             for source, target in zip(fields[:LEVELS], ys):
                 size = target.shape[2] - 2 * PAD
@@ -364,18 +392,18 @@
             return carry
 
         lax.fori_loop(0, tiles, reduce_tile, 0, unroll=UNROLL)
-        return carry
-
-    late = c >= cols_n // 2
+
+    late = c >= middle
     inner = x.at[:, 1 : tiles - 1, PAD : PAD + height]
     pltpu.make_async_copy(inner, inner, x_sem.at[2]).wait()
-    lax.fori_loop(0, bands, reduce_band, 0)
-    pl.when(jnp.logical_not(late))(forward)
+    for b in range(bands):
+        reduce_band(b)
+    pl.when(jnp.logical_not(late | direct))(forward)
 
     rest = sum(sizes[1:])
     at = lax.broadcasted_iota(jnp.int32, (128, 128), 1)
 
-    def reduce_columns(b, carry):
+    def reduce_columns(b):
         base = 0
         for k in range(LEVELS):
             for i in range(tiles):
@@ -404,6 +432,16 @@
         o2[b] = two[: sizes[1]]
         o3[b] = three[: sizes[2]]
         o4[b] = four[:, : width >> 4]
+    for b in range(bands):
+        reduce_columns(b)
+
+    @pl.when(direct)
+    def _():
+        v_low.wait_recv()
+        for b in range(bands):
+            vown[b] = vown[b] + jnp.where(row == 7, pltpu.roll(vfrom_high[...], 7 - b, 0), 0.0)
+
+    def finish_columns(b):
         for part, levels in ((0, (0,)), (1, (1, 2, 3))):
             square = jnp.concatenate(
                 [vown[b, :, 128 * part : 128 * part + 128], jnp.zeros((120, 128), jnp.float32)], 0
@@ -418,9 +456,8 @@
                 high_cells = jnp.where(mark == tile - 1, pltpu.roll(value, tile - 8, 1), 0.0)[:, :tile]
                 out[b, :, 0:tile] = out[b, :, 0:tile] + low_cells
                 out[b, :, out.shape[2] - tile :] = out[b, :, out.shape[2] - tile :] + high_cells
-        return carry
-
-    lax.fori_loop(0, bands, reduce_columns, 0)
+    for b in range(bands):
+        finish_columns(b)
 
     above = lax.broadcasted_iota(jnp.int32, (8, 128), 1) < 8
     z_arrive()
@@ -428,12 +465,21 @@
         low_rows[b] = jnp.where(has_low_row, zfrom_low[b], 0.0)
         high_rows[b] = jnp.where(has_high_row, zfrom_high[b], 0.0)
     e_arrive()
+    from_low, from_high = direct & has_low_row, direct & has_high_row
+    pl.when(from_low)(diagonals[0].wait_recv)
+    pl.when(from_high)(diagonals[1].wait_recv)
+    diagonal = jnp.where(
+        above, jnp.where(from_low, dfrom_low[...], 0.0), jnp.where(from_high, dfrom_high[...], 0.0)
+    )
+    last_row = lax.broadcasted_iota(jnp.int32, (8, 128), 0) == 7
     for b in range(bands):
         corners[b] = jnp.where(
             above,
             jnp.where(has_low_row, efrom_low[b], 0.0),
             jnp.where(has_high_row, efrom_high[b], 0.0),
-        )
+        ) + jnp.where(last_row, pltpu.roll(diagonal, 7 - b, 0), 0.0)
+    pl.when(sends_diagonal & has_high_row)(diagonals[0].wait_send)
+    pl.when(sends_diagonal & has_low_row)(diagonals[1].wait_send)
     e_sent()
     z_sent()
     v_sent()
@@ -512,8 +558,9 @@
         scratch += [vmem(bands, 8, width // 4)] * 4
         scratch += [vmem(bands, 8, 128)] * 3
         scratch += [vmem(bands, 8, height + 128)] + [vmem(8, height + 128)] * 4
+        scratch += [vmem(8, 128)] * 2
         scratch += [
-            pltpu.SemaphoreType.DMA(n) for n in ((2,), (3,), (4,), (4,), (4,), (4,))
+            pltpu.SemaphoreType.DMA(n) for n in ((2,), (3,), (4,), (4,), (4,), (4,), (4,))
         ]
         scratch += [pltpu.SemaphoreType.REGULAR]
         extra = [(bands, 8, width // 4)] * 2 + [(bands, 8, 128)]

time: 12.1 us -> 10.7 us (0.88)
  the two profiles are of different devices: /device:TPU:71 before, /device:TPU:32 now
where the time goes in v6:
time: 10.7 us; the launch traced here: 10.6 us
  Pallas kernels  9.92 us (93%)
  between operations  0.64 us (6%)
    pallas_call x1, Pallas kernels, local(): pl.pallas_call(functools.partial(pyramid_kernel, rows_n, cols_n), out_sha...  8.84 us
    pallas_call x1, Pallas kernels, local(): pl.pallas_call(store_kernel, out_shape=[jax.ShapeDtypeStruct(s, f32) for...  1.08 us

profile of v6, /device:TPU:32, one launch (start us, length us, event | category | flops | bytes accessed | tf_op | source)
XLA Modules:
  0.0 10.6 jit_solution(1931219353682850241)
XLA Ops:
  0.6 8.8 %pyramid.1 = (f32[3,128,512]{2,1,0:T(8,128)S(1)}, f32[3,64,256]{2,1,0:T(8,128)S(1)}, f32[3,32,128]{2,1,0:T(8,128)S(1)}, f32[3,16,64]{2,1,0:T(8,128)S(1)}, f32[3,...) custom-call(f32[3,256,1024]{2,1,0:T(8,128)} %x_hbm.1, ...), custom_call_target="tpu_custom_call" | custom-call | tf_op jit(solution)/shard_map/pyramid/pallas_call | solution.py:567
  9.5 1.1 %store.1 = (f32[3,128,512]{2,1,0:T(8,128)}, f32[3,64,256]{2,1,0:T(8,128)}, f32[3,32,128]{2,1,0:T(8,128)}, f32[3,16,64]{2,1,0:T(8,128)}) custom-call(f32[3,128,512]{2,1,0:T(8,128)S(1)} %get-tuple-element.11.a1, f32[3,64,256]{2,1,0:T(8,128)S(1)} %get-tuple-element.12.a2, f32[3,32,128]{2,1,0:T(8,128)S(1)} %get-tuple-element.13.a3, ...), custom_call_target="tpu_custom_call" | custom-call | tf_op jit(solution)/shard_map/store/pallas_call | solution.py:578

commit v7 on v6

--- a/solution.py
+++ b/solution.py
@@ -144,6 +144,21 @@
     sizes = [height >> (k + 1) for k in range(LEVELS)]
     starts = [height - (height >> k) for k in range(LEVELS)]
 
+    def load(source, target, sem):
+        copy = pltpu.make_async_copy(source, target, sem)
+        copy.start()
+        return copy
+
+    def load_tile(i, sem):
+        return load(x_hbm.at[:, :, 128 * i : 128 * i + 128], x.at[:, i, PAD : PAD + height], sem)
+
+    col_loads = [
+        load(ct_hbm.at[place(c, cols_n)], ct, t_sem.at[0]),
+        load_tile(0, x_sem.at[0]),
+        load_tile(tiles - 1, x_sem.at[1]),
+    ]
+    wr_load = load(wr_hbm.at[place(r, rows_n)], wr, t_sem.at[1])
+
     place_in_line = r % 8
     far_high = (place_in_line == 7) & has_high_row
     far_low = (place_in_line == 0) & has_low_row
@@ -171,21 +186,6 @@
         def _(step=step):
             pl.semaphore_signal(barrier, inc=1, device_id={"row": r + step, "col": c + 1}, device_id_type=MESH)
 
-    def load(source, target, sem):
-        copy = pltpu.make_async_copy(source, target, sem)
-        copy.start()
-        return copy
-
-    def load_tile(i, sem):
-        return load(x_hbm.at[:, :, 128 * i : 128 * i + 128], x.at[:, i, PAD : PAD + height], sem)
-
-    col_loads = [
-        load(ct_hbm.at[place(c, cols_n)], ct, t_sem.at[0]),
-        load_tile(0, x_sem.at[0]),
-        load_tile(tiles - 1, x_sem.at[1]),
-    ]
-    wr_load = load(wr_hbm.at[place(r, rows_n)], wr, t_sem.at[1])
-
     for field in fields[:LEVELS]:
         size = field.shape[2] - 2 * PAD
         zeros = jnp.zeros((bands, tiles, PAD, 128), jnp.float32)
@@ -232,7 +232,8 @@
     wr_load.wait()
     high, low = split(raw)
     v = dot(jnp.concatenate([high, low], 0), wr[0])
-    v = v[: raw.shape[0]] + v[raw.shape[0] :] + dot(high, wr[1])
+    v = v[: raw.shape[0]] + v[raw.shape[0] :]
+    v = jnp.concatenate([v[:, :128], v[:, 128:] + dot(high, wr[1, :, 128:])], 1)
     lane = lax.broadcasted_iota(jnp.int32, (8, height + 128), 1)
     row = lax.broadcasted_iota(jnp.int32, (8, height + 128), 0)
     beyond = lane - height
@@ -375,7 +376,9 @@
 
     def reduce_band(b):
         if b == FORWARD:
-            pl.when(direct)(lambda: forward(False))
+            pl.when(direct & jnp.logical_not(after_last))(lambda: forward(False))
+        if b == bands - 1:
+            pl.when(direct & after_last)(lambda: forward(False))
         if b == EARLY:
             pl.when(late)(forward)
         def reduce_tile(i, carry):
@@ -394,6 +397,7 @@
         lax.fori_loop(0, tiles, reduce_tile, 0, unroll=UNROLL)
 
     late = c >= middle
+    after_last = (r == 0) & (c == 1)
     inner = x.at[:, 1 : tiles - 1, PAD : PAD + height]
     pltpu.make_async_copy(inner, inner, x_sem.at[2]).wait()
     for b in range(bands):

time: 10.7 us -> 10.4 us (0.972)
  the two profiles are of different devices: /device:TPU:32 before, /device:TPU:120 now
where the time goes in v7:
time: 10.4 us; the launch traced here: 10.3 us
  Pallas kernels  9.62 us (92%)
  between operations  0.64 us (6%)
    pallas_call x1, Pallas kernels, local(): pl.pallas_call(functools.partial(pyramid_kernel, rows_n, cols_n), out_sha...  8.53 us
    pallas_call x1, Pallas kernels, local(): pl.pallas_call(store_kernel, out_shape=[jax.ShapeDtypeStruct(s, f32) for...  1.08 us

profile of v7, /device:TPU:120, one launch (start us, length us, event | category | flops | bytes accessed | tf_op | source)
XLA Modules:
  0.0 10.3 jit_solution(11366545011567880589)
XLA Ops:
  0.6 8.5 %pyramid.1 = (f32[3,128,512]{2,1,0:T(8,128)S(1)}, f32[3,64,256]{2,1,0:T(8,128)S(1)}, f32[3,32,128]{2,1,0:T(8,128)S(1)}, f32[3,16,64]{2,1,0:T(8,128)S(1)}, f32[3,...) custom-call(f32[3,256,1024]{2,1,0:T(8,128)} %x_hbm.1, ...), custom_call_target="tpu_custom_call" | custom-call | tf_op jit(solution)/shard_map/pyramid/pallas_call | solution.py:571
  9.2 1.1 %store.1 = (f32[3,128,512]{2,1,0:T(8,128)}, f32[3,64,256]{2,1,0:T(8,128)}, f32[3,32,128]{2,1,0:T(8,128)}, f32[3,16,64]{2,1,0:T(8,128)}) custom-call(f32[3,128,512]{2,1,0:T(8,128)S(1)} %get-tuple-element.11.a1, f32[3,64,256]{2,1,0:T(8,128)S(1)} %get-tuple-element.12.a2, f32[3,32,128]{2,1,0:T(8,128)S(1)} %get-tuple-element.13.a3, ...), custom_call_target="tpu_custom_call" | custom-call | tf_op jit(solution)/shard_map/store/pallas_call | solution.py:582

commit v8 on v7

--- a/solution.py
+++ b/solution.py
@@ -14,7 +14,7 @@
 PAD = 8
 ROW_STRIP = 32
 COL_STRIP = 64
-UNROLL = 4
+UNROLL = 8
 DIRECT = 4
 FORWARD = 1
 EARLY = 1
@@ -153,9 +153,9 @@
         return load(x_hbm.at[:, :, 128 * i : 128 * i + 128], x.at[:, i, PAD : PAD + height], sem)
 
     col_loads = [
-        load(ct_hbm.at[place(c, cols_n)], ct, t_sem.at[0]),
         load_tile(0, x_sem.at[0]),
         load_tile(tiles - 1, x_sem.at[1]),
+        load(ct_hbm.at[place(c, cols_n)], ct, t_sem.at[0]),
     ]
     wr_load = load(wr_hbm.at[place(r, rows_n)], wr, t_sem.at[1])
 
@@ -197,13 +197,10 @@
         copy.wait()
     row_loads = [load(rt_hbm.at[place(r, rows_n)], rt, t_sem.at[2])]
     for e, begin in enumerate((0, height - ROW_STRIP)):
-        row_loads.append(
-            load(
-                x_hbm.at[:, begin : begin + ROW_STRIP],
-                strip.at[:, e * ROW_STRIP : (e + 1) * ROW_STRIP],
-                s_sem.at[e],
-            )
-        )
+        load(
+            x_hbm.at[:, begin : begin + ROW_STRIP], strip.at[:, e * ROW_STRIP : (e + 1) * ROW_STRIP], s_sem
+        )
+    row_loads.append(pltpu.make_async_copy(strip, strip, s_sem))
     row_loads.append(load(cc_hbm, cc, t_sem.at[3]))
     for i in range(1, tiles - 1):
         load_tile(i, x_sem.at[2])
@@ -564,7 +561,7 @@
         scratch += [vmem(bands, 8, height + 128)] + [vmem(8, height + 128)] * 4
         scratch += [vmem(8, 128)] * 2
         scratch += [
-            pltpu.SemaphoreType.DMA(n) for n in ((2,), (3,), (4,), (4,), (4,), (4,), (4,))
+            pltpu.SemaphoreType.DMA(n) for n in ((), (3,), (4,), (4,), (4,), (4,), (4,))
         ]
         scratch += [pltpu.SemaphoreType.REGULAR]
         extra = [(bands, 8, width // 4)] * 2 + [(bands, 8, 128)]

time: 10.4 us -> 10.3 us (level)
  no operation moved by 1% of the time
where the time goes in v8:
time: 10.3 us; the launch traced here: 10.2 us
  Pallas kernels  9.58 us (93%)
  between operations  0.64 us (6%)
    pallas_call x1, Pallas kernels, local(): pl.pallas_call(functools.partial(pyramid_kernel, rows_n, cols_n), out_sha...  8.5 us
    pallas_call x1, Pallas kernels, local(): pl.pallas_call(store_kernel, out_shape=[jax.ShapeDtypeStruct(s, f32) for...  1.08 us

profile of v8, /device:TPU:120, one launch (start us, length us, event | category | flops | bytes accessed | tf_op | source)
XLA Modules:
  0.0 10.2 jit_solution(16345604805433136905)
XLA Ops:
  0.6 8.5 %pyramid.1 = (f32[3,128,512]{2,1,0:T(8,128)S(1)}, f32[3,64,256]{2,1,0:T(8,128)S(1)}, f32[3,32,128]{2,1,0:T(8,128)S(1)}, f32[3,16,64]{2,1,0:T(8,128)S(1)}, f32[3,...) custom-call(f32[3,256,1024]{2,1,0:T(8,128)} %x_hbm.1, ...), custom_call_target="tpu_custom_call" | custom-call | tf_op jit(solution)/shard_map/pyramid/pallas_call | solution.py:568
  9.1 1.1 %store.1 = (f32[3,128,512]{2,1,0:T(8,128)}, f32[3,64,256]{2,1,0:T(8,128)}, f32[3,32,128]{2,1,0:T(8,128)}, f32[3,16,64]{2,1,0:T(8,128)}) custom-call(f32[3,128,512]{2,1,0:T(8,128)S(1)} %get-tuple-element.11.a1, f32[3,64,256]{2,1,0:T(8,128)S(1)} %get-tuple-element.12.a2, f32[3,32,128]{2,1,0:T(8,128)S(1)} %get-tuple-element.13.a3, ...), custom_call_target="tpu_custom_call" | custom-call | tf_op jit(solution)/shard_map/store/pallas_call | solution.py:579
